TPU v7x, 512 devices: a whole 4x8x8 slice. The times are simulated.
512 devices in a mesh: grp: 16 (over y, core), pts: 32 (over x, z).
Axes of the slice: x: 4, y: 8, z: 8, core: 2. Of those that a mesh axis runs over, the one named last changes fastest.
Arguments:
- embeddings: bfloat16 [262144, 768], P(('grp', 'pts')), may hold values from -16 to 16
- frequencies: bfloat16 [768, 256], replicated, may hold values from -6 to 6
- phases: float32 [9, 256], replicated, may hold values from -3.140625 to 3.140625
- solution: float32 [32, 262144], P(None, ('grp', 'pts')), may hold values from -6 to 6
- residual: float32 [32, 262144], P(None, ('grp', 'pts')), may hold values from -100 to 100
- direction: float32 [32, 262144], P(None, ('grp', 'pts')), may hold values from -100 to 100
Outputs:
- new_solution: float32 [32, 262144], P(None, ('grp', 'pts'))
- new_residual: float32 [32, 262144], P(None, ('grp', 'pts'))
- new_direction: float32 [32, 262144], P(None, ('grp', 'pts'))
All inputs are finite; a program needn't handle non-finite values.
Results may differ from a plain program's by a relative error of at most 0.0003.
Values sent between devices are 32-bit elements; how exact they have to be, the bound alone decides.
No kernel may reach another device: no remote copies, remote signals or barrier semaphores. Data moves between devices by JAX's collectives and lax.ppermute only.
A program may use at most 64 MiB of HBM per device.

v0:
```python
import math

import jax
import jax.numpy as jnp
import numpy as np
from jax import lax
from jax.experimental import pallas as pl
from jax.experimental.pallas import tpu as pltpu
from jax.sharding import Mesh
from jax.sharding import PartitionSpec as P

AXES = ("y", "c", "x", "z")
LEAF, EMBED, RANK, ROWS, LEVELS = 512, 768, 256, 32, 9
PTS, GRP = 32, 16
RIDGE = 0.5
HALF = LEAF // 2
CHUNK = 32

f32 = jnp.float32
bf16 = jnp.bfloat16
highest = lax.Precision.HIGHEST


def cosine_coefficients():
    cheb = np.polynomial.chebyshev
    nodes = np.cos(np.pi * (np.arange(64) + 0.5) / 64)
    squares = np.pi**2 * (nodes + 1.0) / 2.0
    series = cheb.chebfit(nodes, np.cos(np.sqrt(squares)), 7)
    poly = np.polynomial.Polynomial(cheb.cheb2poly(series))
    shifted = poly(np.polynomial.Polynomial([-1.0, 2.0 / np.pi**2]))
    return [float(value) for value in shifted.coef * math.sqrt(2.0 / RANK)]


COSINE = cosine_coefficients()
TURN_HIGH = 6.28125
TURN_LOW = 2.0 * math.pi - TURN_HIGH


def scaled_cosine(angle):
    turns = jnp.round(angle * (1.0 / (2.0 * math.pi)))
    reduced = (angle - turns * TURN_HIGH) - turns * TURN_LOW
    square = reduced * reduced
    value = jnp.full_like(square, COSINE[-1])
    for coefficient in COSINE[-2::-1]:
        value = value * square + coefficient
    return value


def split(value):
    high = value.astype(bf16)
    return high, (value - high.astype(f32)).astype(bf16)


def mm(left, right):
    return jnp.dot(left, right, preferred_element_type=f32)


def mm_t(left, right, precision=None):
    return lax.dot_general(
        left, right, (((1,), (1,)), ((), ())), preferred_element_type=f32, precision=precision
    )


def mm3(left, right):
    return mm(left[0], right[0]) + (mm(left[0], right[1]) + mm(left[1], right[0]))


def mm6(left, right):
    return jnp.dot(left, right, preferred_element_type=f32, precision=highest)


def length_scale(depth):
    return 0.5 * 2.0 ** (depth / 8.0)


def features_kernel(emb, freq, phase, direction, feat, part_first, part, proj, high, low):
    proj[...] = mm(emb[...], freq[...])

    def chunk(step, carry):
        rows = pl.ds(pl.multiple_of(step * CHUNK, CHUNK), CHUNK)
        block = proj[rows, :]
        for level in range(LEVELS):
            angle = block * (1.0 / length_scale(level + 1)) + phase[level : level + 1, :]
            value = scaled_cosine(angle)
            feat[level, rows, :] = value
            high_part, low_part = split(value)
            high[level, rows, :] = high_part
            low[level, rows, :] = low_part
        return carry

    lax.fori_loop(0, LEAF // CHUNK, chunk, 0)
    direction_high, direction_low = split(direction[...])
    stacked = jnp.concatenate([direction_high, direction_low], axis=0)
    for level in range(LEVELS):
        both = mm(stacked, high[level])
        total = both[:ROWS] + (both[ROWS:] + mm(direction_high, low[level]))
        if level == 0:
            part_first[...] = total
        else:
            slot = 2 * (level - 1)
            part[pl.ds(slot, ROWS, stride=16), :] = total[:, :128]
            part[pl.ds(slot + 1, ROWS, stride=16), :] = total[:, 128:]


def eye_block():
    row = lax.broadcasted_iota(jnp.int32, (HALF, HALF), 0)
    column = lax.broadcasted_iota(jnp.int32, (HALF, HALF), 1)
    return jnp.where(row == column, 1.0, 0.0).astype(f32)


def inverse_block(block, largest):
    eye = eye_block()
    start = 2.0 / (RIDGE + largest)
    scale = jnp.minimum((largest + RIDGE) / jnp.maximum(largest - RIDGE, 1e-3), 1e4)
    error = eye - start * block
    inverse = None
    for step in range(6):
        double = 2.0 * scale * scale
        gain = double / (double - 1.0)
        error_parts = split(error)
        if step == 0:
            inverse = (gain * start) * (eye + error)
        else:
            inverse = gain * (inverse + mm3(split(inverse), error_parts))
        if step < 5:
            error = gain * mm3(error_parts, error_parts) - (gain / double) * eye
            scale = jnp.minimum(double - 1.0, 1e4)
    block_parts = split(block)
    for step in range(3):
        if step < 2:
            error = eye - mm3(block_parts, split(inverse))
        else:
            error = eye - mm6(block, inverse)
        inverse_high, inverse_low = split(inverse)
        if step < 1:
            inverse = inverse + mm3((inverse_high, inverse_low), split(error))
        else:
            inverse = inverse + mm(inverse_high, error.astype(bf16))
    return inverse


def leaf_kernel(emb, direction, residual, inv, solved, near, matrix):
    points = emb[...]
    wide = points.astype(f32)
    square_high, square_low = split(wide * wide)
    ones_left = jnp.ones((8, EMBED), bf16)
    ones_right = jnp.ones((EMBED, 128), bf16)
    along = (mm_t(ones_left, square_high) + mm_t(ones_left, square_low))[:1, :]
    down = (mm(square_high, ones_right) + mm(square_low, ones_right))[:, :1]
    inv[...] = down + along
    matrix[...] = mm_t(points, points)

    def chunk(step, carry):
        begin = pl.multiple_of(step * CHUNK, CHUNK)
        rows = pl.ds(begin, CHUNK)
        distances = inv[rows, :] - 2.0 * matrix[rows, :]
        value = math.sqrt(RANK / LEAF) * jnp.exp(distances * (-1.0 / 0.5))
        row = begin + lax.broadcasted_iota(jnp.int32, (CHUNK, LEAF), 0)
        column = lax.broadcasted_iota(jnp.int32, (CHUNK, LEAF), 1)
        matrix[rows, :] = value + jnp.where(row == column, RIDGE, 0.0)
        return carry

    lax.fori_loop(0, LEAF // CHUNK, chunk, 0)
    near[...] = mm6(direction[...], matrix[...])
    sums = jnp.sum(matrix[...], axis=0, keepdims=True)
    largest = jnp.max(sums, axis=1, keepdims=True)
    corner = matrix[:HALF, :HALF]
    side = matrix[:HALF, HALF:]
    first = inverse_block(corner, largest)
    across = mm6(first, side)
    across_t = jnp.transpose(across)
    schur = matrix[HALF:, HALF:] - mm6(across_t, side)
    second = inverse_block(schur, largest)
    lower = -mm6(second, across_t)
    inv[:HALF, :HALF] = first - mm6(across, lower)
    inv[HALF:, :HALF] = lower
    inv[:HALF, HALF:] = jnp.transpose(lower)
    inv[HALF:, HALF:] = second
    solved[...] = mm6(residual[...], inv[...])


def middle_send_kernel(received, out):
    total = received[0, 8:16, :]
    for source in range(1, PTS):
        total = total + received[source, 8:16, :]
    for target in range(GRP):
        out[target] = total


def row_select(tiles):
    row = lax.broadcasted_iota(jnp.int32, (8, 128), 0)
    return jnp.where(row < 2, tiles[0], jnp.where(row < 4, tiles[1], jnp.where(row < 6, tiles[2], tiles[3])))


def middle_return_kernel(place, received, wide, out):
    sums = [received[source, 0:8, :] for source in range(PTS)]
    stages = []
    for _ in range(5):
        sums = [sums[2 * n] + sums[2 * n + 1] for n in range(len(sums) // 2)]
        stages.append(sums)
    line = place[0]
    upper = []
    for depth in range(4):
        base = (line >> depth) << (depth + 1)
        total = wide[base] + wide[base + 1]
        for source in range(2, 2 ** (depth + 1)):
            total = total + wide[base + source]
        upper.append(total)
    top = row_select(upper)
    for node in range(8):
        low = row_select([stages[1][node], stages[2][node // 2], stages[3][node // 4], stages[4][0]])
        for leaf in range(4):
            out[node * 4 + leaf, 0:8, :] = low
            out[node * 4 + leaf, 8:16, :] = top


def image_kernel(
    own_first, other_first, returned, feat, near, direction, residual, solved, inv, image, shifted, out
):
    spread = near[...]
    for level in range(LEVELS):
        if level == 0:
            total = own_first[...] + other_first[...]
        else:
            slot = 2 * (level - 1)
            total = jnp.concatenate(
                [returned[pl.ds(slot, ROWS, stride=16), :], returned[pl.ds(slot + 1, ROWS, stride=16), :]],
                axis=1,
            )
        weight = math.sqrt(RANK / (LEAF * 2 ** (level + 1)))
        spread = spread + mm_t(total * weight, feat[level], highest)
    image[...] = spread
    moved = mm6(spread, inv[...])
    shifted[...] = moved
    residual_solved = solved[...]
    products = jnp.concatenate(
        [residual[...] * residual_solved, direction[...] * spread, residual_solved * spread, spread * moved], axis=0
    )
    sums = mm_t(jnp.ones((8, LEAF), f32), products, highest)
    out[...] = sums


def sum_spread_kernel(received, out):
    total = received[0]
    for source in range(1, PTS):
        total = total + received[source]
    for target in range(GRP):
        out[target] = total


def finish_kernel(received, solution, residual, direction, solved, image, shifted, new_solution, new_residual, new_direction):
    total = received[0]
    for source in range(1, GRP):
        total = total + received[source]
    row = lax.broadcasted_iota(jnp.int32, (ROWS, 128), 0)
    column = lax.broadcasted_iota(jnp.int32, (ROWS, 128), 1)
    spread = jnp.broadcast_to(total, (ROWS, 128))

    def pick(slot):
        return jnp.sum(jnp.where(column == row + ROWS * slot, spread, 0.0), axis=1, keepdims=True)

    norm_old, curvature, cross, moved = pick(0), pick(1), pick(2), pick(3)
    step = norm_old / curvature
    norm_new = norm_old - step * (2.0 * cross - step * moved)
    ratio = norm_new / norm_old
    direction_value = direction[...]
    new_solution[...] = solution[...] + step * direction_value
    new_residual[...] = residual[...] - step * image[...]
    new_direction[...] = (solved[...] - step * shifted[...]) + ratio * direction_value


def whole(shape, dtype=f32):
    return jax.ShapeDtypeStruct(shape, dtype)


def call(kernel, outs, *args, scratch=(), name=None, scalars=0):
    vmem = pl.BlockSpec(memory_space=pltpu.VMEM)
    smem = pl.BlockSpec(memory_space=pltpu.SMEM)
    single = not isinstance(outs, (tuple, list))
    return pl.pallas_call(
        kernel,
        out_shape=outs,
        in_specs=[smem if n < scalars else vmem for n in range(len(args))],
        out_specs=vmem if single else tuple(vmem for _ in outs),
        scratch_shapes=list(scratch),
        compiler_params=pltpu.CompilerParams(vmem_limit_bytes=50 * 2**20),
        name=name,
    )(*args)


def exchange(value, axes):
    return lax.all_to_all(value, axes, 0, 0, tiled=True)


def body(embeddings, frequencies, phases, solution, residual, direction):
    rows = whole((ROWS, LEAF))
    feat, part_first, part = call(
        features_kernel,
        (whole((LEVELS, LEAF, RANK)), whole((ROWS, RANK)), whole((ROWS * 16, 128))),
        embeddings, frequencies, phases, direction,
        scratch=(
            pltpu.VMEM((LEAF, RANK), f32),
            pltpu.VMEM((LEVELS, LEAF, RANK), bf16),
            pltpu.VMEM((LEVELS, LEAF, RANK), bf16),
        ),
        name="features",
    )
    other_first = lax.ppermute(part_first, "z", [(n, n ^ 1) for n in range(8)])
    received = exchange(part.reshape(ROWS, 16, 128), ("x", "z"))
    inv, solved, near = call(
        leaf_kernel, (whole((LEAF, LEAF)), rows, rows), embeddings, direction, residual,
        scratch=(pltpu.VMEM((LEAF, LEAF), f32),), name="leaf",
    )
    middle = call(middle_send_kernel, whole((GRP, 8, 128)), received, name="middle_send")
    wide = exchange(middle, ("y", "c"))
    place = lax.axis_index("y").astype(jnp.int32).reshape(1)
    back = call(middle_return_kernel, whole((PTS, 16, 128)), place, received, wide, name="middle_return", scalars=1)
    returned = exchange(back, ("x", "z"))
    image, shifted, sums = call(
        image_kernel, (rows, rows, whole((8, 128))),
        part_first, other_first, returned.reshape(PTS * 16, 128), feat, near, direction, residual, solved, inv,
        name="image",
    )
    gathered = exchange(jnp.broadcast_to(sums[None, :1, :], (PTS, 1, 128)), ("x", "z"))
    middle_sums = call(sum_spread_kernel, whole((GRP, 1, 128)), gathered, name="sum_spread")
    totals = exchange(middle_sums, ("y", "c"))
    return call(
        finish_kernel, (rows, rows, rows), totals, solution, residual, direction, solved, image, shifted, name="finish"
    )


def solution(mesh):
    torus = Mesh(mesh.devices.reshape(8, 2, 4, 8), AXES)
    columns = P(None, AXES)
    return jax.shard_map(
        body,
        mesh=torus,
        in_specs=(P(AXES, None), P(), P(), columns, columns, columns),
        out_specs=(columns, columns, columns),
        check_vma=False,
    )
```

profile of v0, /device:TPU:1, one launch (start us, length us, event | category | flops | bytes accessed | tf_op | source)
XLA Modules:
  0.0 116.7 jit_solution(8105472793713745660)
XLA Ops:
  0.6 1.1 copy-done
  1.8 0.8 copy-done.2
  2.6 1.0 copy-done.8
  3.6 0.7 copy-done.10
  4.3 7.1 %features.1 = (f32[9,512,256]{2,1,0:T(8,128)}, f32[32,256]{1,0:T(8,128)S(1)}, f32[512,128]{1,0:T(8,128)S(1)}) custom-call(bf16[512,768]{1,0:T(8,128)(2,1)S(1)} %copy-done, bf16[768,256]{1,0:T(8,128)(2,1)S(1)} %copy-done.8, f32[9,256]{1,0:T(8,128)S(1)} %copy-done.10, f32[32,512]{1,0:T(8,128)S(1)} %copy-done.2), custom_call_target="tpu_custom_call" | custom-call | tf_op jit(solution)/shard_map/features/pallas_call | solution.py:280
  11.4 23.3 %all_to_all.25.received = f32[32,16,128]{2,1,0:T(8,128)S(1)} all-to-all(f32[32,16,128]{2,1,0:T(8,128)S(1)} %bitcast.6), channel_id=1, replica_groups=mesh['y'=8,'c'=2,'x'=4,'z'=8] {'x','z'}, dimensions={0} | all-to-all | bytes 524288 | tf_op jit(solution)/shard_map/all_to_all | solution.py:292
  34.7 0.7 middle_send.1
  35.4 10.8 %all-to-all-start.1 = ((f32[16,8,128]{2,1,0:T(8,128)}), f32[16,8,128]{2,1,0:T(8,128)S(1)}, u32[]{:S(2)}, u32[]{:S(2)}) async-start(f32[16,8,128]{2,1,0:T(8,128)} %middle_send.1), calls=%async_computation.1 | async-start | bytes 131072 | tf_op jit(solution)/shard_map/all_to_all | solution.py:292
  46.2 7.8 %all-to-all-done.1.wide = f32[16,8,128]{2,1,0:T(8,128)S(1)} async-done(((f32[16,8,128]{2,1,0:T(8,128)}), f32[16,8,128]{2,1,0:T(8,128)S(1)}, u32[]{:S(2)}, u32[]{:S(2)}) %all-to-all-start.1) | async-done | bytes 65568 | tf_op jit(solution)/shard_map/all_to_all | solution.py:292
  54.0 0.7 middle_return.1
  54.7 4.1 %all-to-all-start.2 = ((f32[32,16,128]{2,1,0:T(8,128)}), f32[32,16,128]{2,1,0:T(8,128)S(1)}, u32[]{:S(2)}, u32[]{:S(2)}) async-start(f32[32,16,128]{2,1,0:T(8,128)} %middle_return.1), calls=%async_computation.2 | async-start | bytes 524288 | tf_op jit(solution)/shard_map/all_to_all | solution.py:292
  58.8 3.1 %collective-permute-start = (f32[32,256]{1,0:T(8,128)S(1)}, f32[32,256]{1,0:T(8,128)S(1)}, u32[]{:S(2)}, u32[]{:S(2)}) collective-permute-start(f32[32,256]{1,0:T(8,128)S(1)} %get-tuple-element.12.own_first), channel_id=1, source_target_pairs={{0,1},{1,0},{2,3},{3,2},{4,5},{5,4},{6,7},{7,6},{8,9},{9,8},{10,11... | collective-permute-start | bytes 98312 | tf_op jit(solution)/shard_map/ppermute | solution.py:308
  62.0 0.0 copy-start.1
  62.0 1.1 copy-done.1
  63.1 0.8 copy-done.3
  64.0 0.8 copy-done.6
  64.8 13.2 %leaf.1 = (f32[512,512]{1,0:T(8,128)S(1)}, f32[32,512]{1,0:T(8,128)S(1)}, f32[32,512]{1,0:T(8,128)S(1)}) custom-call(bf16[512,768]{1,0:T(8,128)(2,1)S(1)} %copy-done.1, f32[32,512]{1,0:T(8,128)S(1)} %copy-done.3, f32[32,512]{1,0:T(8,128)S(1)} %copy-done.6), custom_call_target="tpu_custom_call" | custom-call | tf_op jit(solution)/shard_map/leaf/pallas_call | solution.py:280
  78.0 0.0 all-to-all-done.2
  78.1 0.8 copy-done.4
  78.9 0.8 copy-done.7
  79.7 7.5 %image.1 = (f32[32,512]{1,0:T(8,128)S(1)}, f32[32,512]{1,0:T(8,128)S(1)}, f32[8,128]{1,0:T(8,128)S(1)}) custom-call(f32[32,256]{1,0:T(8,128)S(1)} %get-tuple-element.12.own_first, f32[32,256]{1,0:T(8,128)S(1)} %collective-permute-done.other_first, f32[512,128]{1,0:T(8,128)S(1)} %bitcast.5, f32[9,512,256]{2,1,0:T(8,128)} %get-tuple-element.14.feat, ...), custom_call_target="tpu_custom_call" | custom-call | tf_op jit(solution)/shard_map/image/pallas_call | solution.py:280
  87.3 16.8 %all_to_all.26.received = f32[32,1,128]{2,1,0:T(1,128)S(1)} all-to-all(f32[32,1,128]{2,1,0:T(1,128)S(1)} %broadcast_in_dim.9), channel_id=1, replica_groups=mesh['y'=8,'c'=2,'x'=4,'z'=8] {'x','z'}, dimensions={0} | all-to-all | bytes 32768 | tf_op jit(solution)/shard_map/all_to_all | solution.py:292
  104.1 11.9 %all_to_all.27.received = f32[16,1,128]{2,1,0:T(1,128)S(1)} all-to-all(f32[16,1,128]{2,1,0:T(1,128)S(1)} %sum_spread.1), channel_id=1, replica_groups=mesh['y'=8,'c'=2,'x'=4,'z'=8] {'y','c'}, dimensions={0} | all-to-all | bytes 16384 | tf_op jit(solution)/shard_map/all_to_all | solution.py:292
  115.9 0.8 finish.1
  (16 shorter events, 0.1 us)
Async XLA Ops:
  0.6 1.1 copy-start
  1.8 0.8 copy-start.2
  2.6 1.0 copy-start.8
  3.6 0.7 copy-start.10
  11.4 104.5 %copy-start.5 = (f32[32,512]{1,0:T(8,128)S(1)}, f32[32,512]{1,0:T(8,128)}, u32[]{:S(2)}) copy-start(f32[32,512]{1,0:T(8,128)} %direction.7) | copy-start | bytes 196612
  11.4 104.5 %copy-start.9 = (f32[32,512]{1,0:T(8,128)S(1)}, f32[32,512]{1,0:T(8,128)}, u32[]{:S(2)}) copy-start(f32[32,512]{1,0:T(8,128)} %solution.1) | copy-start | bytes 196612
  35.4 18.6 %all-to-all-start.1 = ((f32[16,8,128]{2,1,0:T(8,128)}), f32[16,8,128]{2,1,0:T(8,128)S(1)}, u32[]{:S(2)}, u32[]{:S(2)}) async-start(f32[16,8,128]{2,1,0:T(8,128)} %middle_send.1), calls=%async_computation.1 | async-start | bytes 131072 | tf_op jit(solution)/shard_map/all_to_all | solution.py:292
  54.7 23.3 %all-to-all-start.2 = ((f32[32,16,128]{2,1,0:T(8,128)}), f32[32,16,128]{2,1,0:T(8,128)S(1)}, u32[]{:S(2)}, u32[]{:S(2)}) async-start(f32[32,16,128]{2,1,0:T(8,128)} %middle_return.1), calls=%async_computation.2 | async-start | bytes 524288 | tf_op jit(solution)/shard_map/all_to_all | solution.py:292
  58.8 19.2 %collective-permute-start = (f32[32,256]{1,0:T(8,128)S(1)}, f32[32,256]{1,0:T(8,128)S(1)}, u32[]{:S(2)}, u32[]{:S(2)}) collective-permute-start(f32[32,256]{1,0:T(8,128)S(1)} %get-tuple-element.12.own_first), channel_id=1, source_target_pairs={{0,1},{1,0},{2,3},{3,2},{4,5},{5,4},{6,7},{7,6},{8,9},{9,8},{10,11... | collective-permute-start | bytes 98312 | tf_op jit(solution)/shard_map/ppermute | solution.py:308
  62.0 1.1 copy-start.1
  63.1 0.8 copy-start.3
  64.0 0.8 copy-start.6
  78.1 0.8 copy-start.4
  78.9 0.8 copy-start.7
where the time goes:
time: 118 us; the launch traced here: 117 us
  blocking collectives  51.9 us (44%)
  Pallas kernels  30 us (25%)
  starting transfers between devices  18.1 us (15%)
  local copies, waits for them, and re-layouts  8.21 us (7%)
  waiting for transfers between devices  7.79 us (7%)
    all_to_all x3, blocking collectives, exchange(): return lax.all_to_all(value, axes, 0, 0, tiled=True)  51.9 us
    pallas_call x7, Pallas kernels, call(): pl.pallas_call(kernel, out_shape=outs, in_specs=[smem if n < scalars else...  30 us
    all_to_all x2, starting transfers between devices, exchange(): return lax.all_to_all(value, axes, 0, 0, tiled=True)  15 us
    unnamed x22, local copies, waits for them, and re-layouts  8.17 us
    all_to_all x2, waiting for transfers between devices, exchange(): return lax.all_to_all(value, axes, 0, 0, tiled=True)  7.79 us
    ppermute x1, starting transfers between devices, body(): other_first = lax.ppermute(part_first, 'z', [(n, n ^ 1) for n in range(8)])  3.14 us
  transfers between devices with their start and end apart: 3, of which 1 were waited for; matrix products, arithmetic and copies ran while one was open for 0% of the time, Pallas kernels for 11%

commit v1 on v0

--- a/solution.py
+++ b/solution.py
@@ -65,6 +65,22 @@
     return mm(left[0], right[0]) + (mm(left[0], right[1]) + mm(left[1], right[0]))
 
 
+def planes(value):
+    high = value.astype(bf16)
+    rest = value - high.astype(f32)
+    middle = rest.astype(bf16)
+    return high, middle, (rest - middle.astype(f32)).astype(bf16)
+
+
+def six_products(left, right, product):
+    rows = left[0].shape[0]
+    first = product(jnp.concatenate(left, axis=0), right[0])
+    second = product(jnp.concatenate(left[:2], axis=0), right[1])
+    third = product(left[0], right[2])
+    small = third + second[rows:] + first[2 * rows :]
+    return first[:rows] + ((first[rows : 2 * rows] + second[:rows]) + small)
+
+
 def mm6(left, right):
     return jnp.dot(left, right, preferred_element_type=f32, precision=highest)
 
@@ -73,7 +89,20 @@
     return 0.5 * 2.0 ** (depth / 8.0)
 
 
-def features_kernel(emb, freq, phase, direction, feat, part_first, part, proj, high, low):
+def features_kernel(
+    emb_in, freq_in, phase_in, direction_in, feat, part_first, part,
+    emb, freq, phase, direction, proj, keep, high, low, sems,
+):
+    loads = [
+        pltpu.make_async_copy(source, target, sems.at[n])
+        for n, (source, target) in enumerate(
+            ((emb_in, emb), (freq_in, freq), (phase_in, phase), (direction_in, direction))
+        )
+    ]
+    for load in loads:
+        load.start()
+    for load in loads:
+        load.wait()
     proj[...] = mm(emb[...], freq[...])
 
     def chunk(step, carry):
@@ -82,10 +111,11 @@
         for level in range(LEVELS):
             angle = block * (1.0 / length_scale(level + 1)) + phase[level : level + 1, :]
             value = scaled_cosine(angle)
-            feat[level, rows, :] = value
+            keep[level, rows, :] = value
             high_part, low_part = split(value)
             high[level, rows, :] = high_part
             low[level, rows, :] = low_part
+        pltpu.make_async_copy(keep.at[:, rows, :], feat.at[:, rows, :], sems.at[4]).start()
         return carry
 
     lax.fori_loop(0, LEAF // CHUNK, chunk, 0)
@@ -100,6 +130,7 @@
             slot = 2 * (level - 1)
             part[pl.ds(slot, ROWS, stride=16), :] = total[:, :128]
             part[pl.ds(slot + 1, ROWS, stride=16), :] = total[:, 128:]
+    pltpu.make_async_copy(keep, feat, sems.at[4]).wait()
 
 
 def eye_block():
@@ -139,7 +170,18 @@
     return inverse
 
 
-def leaf_kernel(emb, direction, residual, inv, solved, near, matrix):
+def leaf_first_kernel(
+    emb_in, direction_in, after, near, first_out, across_out, schur_out, largest_out,
+    emb, direction, grid, matrix, sems,
+):
+    loads = [
+        pltpu.make_async_copy(emb_in, emb, sems.at[0]),
+        pltpu.make_async_copy(direction_in, direction, sems.at[1]),
+    ]
+    for load in loads:
+        load.start()
+    for load in loads:
+        load.wait()
     points = emb[...]
     wide = points.astype(f32)
     square_high, square_low = split(wide * wide)
@@ -147,13 +189,13 @@
     ones_right = jnp.ones((EMBED, 128), bf16)
     along = (mm_t(ones_left, square_high) + mm_t(ones_left, square_low))[:1, :]
     down = (mm(square_high, ones_right) + mm(square_low, ones_right))[:, :1]
-    inv[...] = down + along
+    grid[...] = down + along
     matrix[...] = mm_t(points, points)
 
     def chunk(step, carry):
         begin = pl.multiple_of(step * CHUNK, CHUNK)
         rows = pl.ds(begin, CHUNK)
-        distances = inv[rows, :] - 2.0 * matrix[rows, :]
+        distances = grid[rows, :] - 2.0 * matrix[rows, :]
         value = math.sqrt(RANK / LEAF) * jnp.exp(distances * (-1.0 / 0.5))
         row = begin + lax.broadcasted_iota(jnp.int32, (CHUNK, LEAF), 0)
         column = lax.broadcasted_iota(jnp.int32, (CHUNK, LEAF), 1)
@@ -164,19 +206,30 @@
     near[...] = mm6(direction[...], matrix[...])
     sums = jnp.sum(matrix[...], axis=0, keepdims=True)
     largest = jnp.max(sums, axis=1, keepdims=True)
-    corner = matrix[:HALF, :HALF]
+    largest_out[...] = jnp.broadcast_to(largest, (8, 128))
     side = matrix[:HALF, HALF:]
-    first = inverse_block(corner, largest)
+    first = inverse_block(matrix[:HALF, :HALF], largest)
     across = mm6(first, side)
-    across_t = jnp.transpose(across)
-    schur = matrix[HALF:, HALF:] - mm6(across_t, side)
-    second = inverse_block(schur, largest)
-    lower = -mm6(second, across_t)
-    inv[:HALF, :HALF] = first - mm6(across, lower)
-    inv[HALF:, :HALF] = lower
-    inv[:HALF, HALF:] = jnp.transpose(lower)
-    inv[HALF:, HALF:] = second
-    solved[...] = mm6(residual[...], inv[...])
+    first_out[...] = first
+    across_out[...] = across
+    schur_out[...] = matrix[HALF:, HALF:] - mm6(jnp.transpose(across), side)
+
+
+def leaf_second_kernel(first, across_in, schur, largest, residual_in, after, solved, inv, residual, sem):
+    load = pltpu.make_async_copy(residual_in, residual, sem.at[0])
+    load.start()
+    across = across_in[...]
+    second = inverse_block(schur[...], largest[:1, :1])
+    lower = -mm6(second, jnp.transpose(across))
+    top = first[...] - mm6(across, lower)
+    left = jnp.concatenate([top, lower], axis=0)
+    right = jnp.concatenate([jnp.transpose(lower), second], axis=0)
+    for n, plane in enumerate(planes(left)):
+        inv[n, :, :HALF] = plane
+    for n, plane in enumerate(planes(right)):
+        inv[n, :, HALF:] = plane
+    load.wait()
+    solved[...] = six_products(planes(residual[...]), [inv[n] for n in range(3)], mm)
 
 
 def middle_send_kernel(received, out):
@@ -192,7 +245,7 @@
     return jnp.where(row < 2, tiles[0], jnp.where(row < 4, tiles[1], jnp.where(row < 6, tiles[2], tiles[3])))
 
 
-def middle_return_kernel(place, received, wide, out):
+def middle_return_kernel(place, received, wide, after, out):
     sums = [received[source, 0:8, :] for source in range(PTS)]
     stages = []
     for _ in range(5):
@@ -215,8 +268,14 @@
 
 
 def image_kernel(
-    own_first, other_first, returned, feat, near, direction, residual, solved, inv, image, shifted, out
+    own_first, other_first, returned, feat_in, near, direction_in, residual_in, solved, inv, image, shifted, out,
+    feat, direction, residual, sems,
 ):
+    loads = [pltpu.make_async_copy(feat_in.at[n], feat.at[n], sems.at[n]) for n in range(LEVELS)]
+    loads.append(pltpu.make_async_copy(direction_in, direction, sems.at[LEVELS]))
+    loads.append(pltpu.make_async_copy(residual_in, residual, sems.at[LEVELS + 1]))
+    for load in loads:
+        load.start()
     spread = near[...]
     for level in range(LEVELS):
         if level == 0:
@@ -228,16 +287,19 @@
                 axis=1,
             )
         weight = math.sqrt(RANK / (LEAF * 2 ** (level + 1)))
-        spread = spread + mm_t(total * weight, feat[level], highest)
+        loads[level].wait()
+        spread = spread + six_products(planes(total * weight), planes(feat[level]), mm_t)
     image[...] = spread
-    moved = mm6(spread, inv[...])
+    moved = six_products(planes(spread), [inv[n] for n in range(3)], mm)
     shifted[...] = moved
-    residual_solved = solved[...]
+    loads[LEVELS].wait()
+    loads[LEVELS + 1].wait()
+    first = solved[...]
     products = jnp.concatenate(
-        [residual[...] * residual_solved, direction[...] * spread, residual_solved * spread, spread * moved], axis=0
-    )
-    sums = mm_t(jnp.ones((8, LEAF), f32), products, highest)
-    out[...] = sums
+        [residual[...] * first, direction[...] * spread, first * spread, spread * moved], axis=0
+    )
+    folded = products[:, :128] + products[:, 128:256] + (products[:, 256:384] + products[:, 384:])
+    out[...] = jnp.sum(jnp.transpose(folded), axis=0, keepdims=True)
 
 
 def sum_spread_kernel(received, out):
@@ -273,15 +335,24 @@
     return jax.ShapeDtypeStruct(shape, dtype)
 
 
-def call(kernel, outs, *args, scratch=(), name=None, scalars=0):
+def call(kernel, outs, *args, scratch=(), name=None, hbm=(), scalars=0, hbm_out=()):
     vmem = pl.BlockSpec(memory_space=pltpu.VMEM)
     smem = pl.BlockSpec(memory_space=pltpu.SMEM)
+    far = pl.BlockSpec(memory_space=pltpu.HBM)
+    anywhere = pl.BlockSpec(memory_space=pl.ANY)
     single = not isinstance(outs, (tuple, list))
+    kinds = {"hbm": far, "any": anywhere}
+    specs = [smem if n < scalars else vmem for n in range(len(args))]
+    args = list(args)
+    for place, kind in hbm:
+        specs[place] = kinds[kind]
+        if kind == "hbm":
+            args[place] = pltpu.with_memory_space_constraint(args[place], pltpu.HBM)
     return pl.pallas_call(
         kernel,
         out_shape=outs,
-        in_specs=[smem if n < scalars else vmem for n in range(len(args))],
-        out_specs=vmem if single else tuple(vmem for _ in outs),
+        in_specs=specs,
+        out_specs=vmem if single else tuple(far if n in hbm_out else vmem for n in range(len(outs))),
         scratch_shapes=list(scratch),
         compiler_params=pltpu.CompilerParams(vmem_limit_bytes=50 * 2**20),
         name=name,
@@ -294,34 +365,60 @@
 
 def body(embeddings, frequencies, phases, solution, residual, direction):
     rows = whole((ROWS, LEAF))
+    half = whole((HALF, HALF))
+    leaf_points = pltpu.VMEM((LEAF, EMBED), bf16)
+    leaf_rows = pltpu.VMEM((ROWS, LEAF), f32)
+    panel = pltpu.VMEM((LEVELS, LEAF, RANK), f32)
     feat, part_first, part = call(
         features_kernel,
         (whole((LEVELS, LEAF, RANK)), whole((ROWS, RANK)), whole((ROWS * 16, 128))),
         embeddings, frequencies, phases, direction,
+        hbm=[(n, "hbm") for n in range(4)],
+        hbm_out=(0,),
         scratch=(
+            leaf_points,
+            pltpu.VMEM((EMBED, RANK), bf16),
+            pltpu.VMEM((LEVELS, RANK), f32),
+            leaf_rows,
             pltpu.VMEM((LEAF, RANK), f32),
+            panel,
             pltpu.VMEM((LEVELS, LEAF, RANK), bf16),
             pltpu.VMEM((LEVELS, LEAF, RANK), bf16),
+            pltpu.SemaphoreType.DMA((5,)),
         ),
         name="features",
     )
     other_first = lax.ppermute(part_first, "z", [(n, n ^ 1) for n in range(8)])
     received = exchange(part.reshape(ROWS, 16, 128), ("x", "z"))
-    inv, solved, near = call(
-        leaf_kernel, (whole((LEAF, LEAF)), rows, rows), embeddings, direction, residual,
-        scratch=(pltpu.VMEM((LEAF, LEAF), f32),), name="leaf",
-    )
     middle = call(middle_send_kernel, whole((GRP, 8, 128)), received, name="middle_send")
     wide = exchange(middle, ("y", "c"))
+    near, first, across, schur, largest = call(
+        leaf_first_kernel, (rows, half, half, half, whole((8, 128))), embeddings, direction, middle,
+        hbm=[(0, "hbm"), (1, "hbm"), (2, "any")],
+        scratch=(
+            leaf_points, leaf_rows, pltpu.VMEM((LEAF, LEAF), f32), pltpu.VMEM((LEAF, LEAF), f32),
+            pltpu.SemaphoreType.DMA((2,)),
+        ),
+        name="leaf_first",
+    )
     place = lax.axis_index("y").astype(jnp.int32).reshape(1)
-    back = call(middle_return_kernel, whole((PTS, 16, 128)), place, received, wide, name="middle_return", scalars=1)
+    back = call(
+        middle_return_kernel, whole((PTS, 16, 128)), place, received, wide, largest,
+        hbm=[(3, "any")], scalars=1, name="middle_return",
+    )
     returned = exchange(back, ("x", "z"))
+    solved, inv = call(
+        leaf_second_kernel, (rows, whole((3, LEAF, LEAF), bf16)), first, across, schur, largest, residual, back,
+        hbm=[(4, "hbm"), (5, "any")], scratch=(leaf_rows, pltpu.SemaphoreType.DMA((1,))), name="leaf_second",
+    )
     image, shifted, sums = call(
-        image_kernel, (rows, rows, whole((8, 128))),
+        image_kernel, (rows, rows, whole((1, 128))),
         part_first, other_first, returned.reshape(PTS * 16, 128), feat, near, direction, residual, solved, inv,
+        hbm=[(3, "hbm"), (5, "hbm"), (6, "hbm")],
+        scratch=(panel, leaf_rows, leaf_rows, pltpu.SemaphoreType.DMA((LEVELS + 2,))),
         name="image",
     )
-    gathered = exchange(jnp.broadcast_to(sums[None, :1, :], (PTS, 1, 128)), ("x", "z"))
+    gathered = exchange(jnp.broadcast_to(sums[None], (PTS, 1, 128)), ("x", "z"))
     middle_sums = call(sum_spread_kernel, whole((GRP, 1, 128)), gathered, name="sum_spread")
     totals = exchange(middle_sums, ("y", "c"))
     return call(

time: 118 us -> 104 us (0.88)
  local copies, waits for them, and re-layouts: 8.21 us -> 0.03 us
  waiting for transfers between devices: 7.79 us -> 1.23 us
  blocking collectives: 51.9 us -> 55.1 us
  Pallas kernels: 30 us -> 27.8 us
    unnamed x22 -> x6, local copies, waits for them, and re-layouts: 8.17 us -> 0.02 us
    all_to_all x2, waiting for transfers between devices: 7.79 us -> 1.23 us  [exchange(): return lax.all_to_all(value, axes, 0, 0, tiled=True)]
    all_to_all x3, blocking collectives: 51.9 us -> 55.1 us  [exchange(): return lax.all_to_all(value, axes, 0, 0, tiled=True)]
    pallas_call x7 -> x8, Pallas kernels: 30 us -> 27.8 us  [call(): pl.pallas_call(kernel, out_shape=outs, in_specs=specs, out_specs=vmem if...]
  transfers between devices with their start and end apart: 3 -> 3, of which waited for: 1 -> 1; matrix products, arithmetic and copies ran while one was open for 0% -> 0% of each run, Pallas kernels for 11% -> 14%
where the time goes in v1:
time: 104 us; the launch traced here: 103 us
  blocking collectives  55.1 us (53%)
  Pallas kernels  27.8 us (27%)
  starting transfers between devices  18.3 us (18%)
  waiting for transfers between devices  1.23 us (1%)
    all_to_all x3, blocking collectives, exchange(): return lax.all_to_all(value, axes, 0, 0, tiled=True)  55.1 us
    pallas_call x8, Pallas kernels, call(): pl.pallas_call(kernel, out_shape=outs, in_specs=specs, out_specs=vmem if...  27.8 us
    all_to_all x2, starting transfers between devices, exchange(): return lax.all_to_all(value, axes, 0, 0, tiled=True)  15 us
    ppermute x1, starting transfers between devices, body(): other_first = lax.ppermute(part_first, 'z', [(n, n ^ 1) for n in range(8)])  3.32 us
  transfers between devices with their start and end apart: 3, of which 1 were waited for; matrix products, arithmetic and copies ran while one was open for 0% of the time, Pallas kernels for 14%

profile of v1, /device:TPU:1, one launch (start us, length us, event | category | flops | bytes accessed | tf_op | source)
XLA Modules:
  0.0 103.1 jit_solution(6196681450118416257)
XLA Ops:
  0.6 7.2 %features.1 = (f32[9,512,256]{2,1,0:T(8,128)}, f32[32,256]{1,0:T(8,128)S(1)}, f32[512,128]{1,0:T(8,128)S(1)}) custom-call(bf16[512,768]{1,0:T(8,128)(2,1)} %emb_in.3, bf16[768,256]{1,0:T(8,128)(2,1)} %freq_in.1, f32[9,256]{1,0:T(8,128)} %phase_in.1, f32[32,512]{1,0:T(8,128)} %direction.1), custom_call_target="tpu_custom_call" | custom-call | tf_op jit(solution)/shard_map/features/pallas_call | solution.py:351
  7.8 23.2 %all_to_all.25.received = f32[32,16,128]{2,1,0:T(8,128)S(1)} all-to-all(f32[32,16,128]{2,1,0:T(8,128)S(1)} %bitcast.5), channel_id=1, replica_groups=mesh['y'=8,'c'=2,'x'=4,'z'=8] {'x','z'}, dimensions={0} | all-to-all | bytes 524288 | tf_op jit(solution)/shard_map/all_to_all | solution.py:363
  31.0 0.7 middle_send.1.after
  31.7 10.8 %all-to-all-start.1 = ((f32[16,8,128]{2,1,0:T(8,128)}), f32[16,8,128]{2,1,0:T(8,128)S(1)}, u32[]{:S(2)}, u32[]{:S(2)}) async-start(f32[16,8,128]{2,1,0:T(8,128)} %middle_send.1.after), calls=%async_computation.1 | async-start | bytes 131072 | tf_op jit(solution)/shard_map/all_to_all | solution.py:363
  42.5 8.8 %leaf_first.1 = (f32[32,512]{1,0:T(8,128)S(1)}, f32[256,256]{1,0:T(8,128)S(1)}, f32[256,256]{1,0:T(8,128)S(1)}, f32[256,256]{1,0:T(8,128)S(1)}, f32[8,128]{1,0:T(8,128)S(1)}) custom-call(bf16[512,768]{1,0:T(8,128)(2,1)} %emb_in.3, f32[32,512]{1,0:T(8,128)} %direction.1, f32[16,8,128]{2,1,0:T(8,128)} %middle_send.1.after), custom_call_target="tpu_custom_call" | custom-call | tf_op jit(solution)/shard_map/leaf_first/pallas_call | solution.py:351
  51.3 0.0 copy-start
  51.3 0.0 copy-start.1
  51.3 0.0 copy-start.2
  51.3 0.0 all-to-all-done.1.wide
  51.3 0.7 middle_return.1.after
  52.1 4.1 %all-to-all-start.2 = ((f32[32,16,128]{2,1,0:T(8,128)}), f32[32,16,128]{2,1,0:T(8,128)S(1)}, u32[]{:S(2)}, u32[]{:S(2)}) async-start(f32[32,16,128]{2,1,0:T(8,128)} %middle_return.1.after), calls=%async_computation.2 | async-start | bytes 524288 | tf_op jit(solution)/shard_map/all_to_all | solution.py:363
  56.2 3.3 %collective-permute-start = (f32[32,256]{1,0:T(8,128)S(1)}, f32[32,256]{1,0:T(8,128)S(1)}, u32[]{:S(2)}, u32[]{:S(2)}) collective-permute-start(f32[32,256]{1,0:T(8,128)S(1)} %get-tuple-element.16.own_first), channel_id=1, source_target_pairs={{0,1},{1,0},{2,3},{3,2},{4,5},{5,4},{6,7},{7,6},{8,9},{9,8},{10,11... | collective-permute-start | bytes 98312 | tf_op jit(solution)/shard_map/ppermute | solution.py:391
  59.5 5.6 %leaf_second.1 = (f32[32,512]{1,0:T(8,128)S(1)}, bf16[3,512,512]{2,1,0:T(8,128)(2,1)S(1)}) custom-call(f32[256,256]{1,0:T(8,128)S(1)} %get-tuple-element.21.first, f32[256,256]{1,0:T(8,128)S(1)} %get-tuple-element.22.across_in, f32[256,256]{1,0:T(8,128)S(1)} %get-tuple-element.23.schur, f32[8,128]{1,0:T(8,128)S(1)} %get-tuple-element.18.after.largest, ...), custom_call_target="tpu_custom_call" | custom-call | tf_op jit(solution)/shard_map/leaf_second/pallas_call | solution.py:351
  65.1 0.0 collective-permute-done.other_first
  65.1 1.2 %all-to-all-done.2 = f32[32,16,128]{2,1,0:T(8,128)S(1)} async-done(((f32[32,16,128]{2,1,0:T(8,128)}), f32[32,16,128]{2,1,0:T(8,128)S(1)}, u32[]{:S(2)}, u32[]{:S(2)}) %all-to-all-start.2) | async-done | bytes 262176 | tf_op jit(solution)/shard_map/all_to_all | solution.py:363
  66.4 4.0 %image.1 = (f32[32,512]{1,0:T(8,128)S(1)}, f32[32,512]{1,0:T(8,128)S(1)}, f32[1,128]{1,0:T(1,128)S(1)}) custom-call(f32[32,256]{1,0:T(8,128)S(1)} %get-tuple-element.16.own_first, f32[32,256]{1,0:T(8,128)S(1)} %collective-permute-done.other_first, f32[512,128]{1,0:T(8,128)S(1)} %bitcast.4, f32[9,512,256]{2,1,0:T(8,128)} %get-tuple-element.19.feat_in, ...), custom_call_target="tpu_custom_call" | custom-call | tf_op jit(solution)/shard_map/image/pallas_call | solution.py:351
  70.4 15.5 %all_to_all.26.received = f32[32,1,128]{2,1,0:T(1,128)S(1)} all-to-all(f32[32,1,128]{2,1,0:T(1,128)S(1)} %broadcast_in_dim.9), channel_id=1, replica_groups=mesh['y'=8,'c'=2,'x'=4,'z'=8] {'x','z'}, dimensions={0} | all-to-all | bytes 32768 | tf_op jit(solution)/shard_map/all_to_all | solution.py:363
  86.0 16.3 %all_to_all.27.received = f32[16,1,128]{2,1,0:T(1,128)S(1)} all-to-all(f32[16,1,128]{2,1,0:T(1,128)S(1)} %sum_spread.1), channel_id=1, replica_groups=mesh['y'=8,'c'=2,'x'=4,'z'=8] {'y','c'}, dimensions={0} | all-to-all | bytes 16384 | tf_op jit(solution)/shard_map/all_to_all | solution.py:363
  102.3 0.0 copy-done
  102.3 0.0 copy-done.1
  102.3 0.0 copy-done.2
  102.3 0.8 finish.1
  (2 shorter events, 0.0 us)
Async XLA Ops:
  31.7 19.6 %all-to-all-start.1 = ((f32[16,8,128]{2,1,0:T(8,128)}), f32[16,8,128]{2,1,0:T(8,128)S(1)}, u32[]{:S(2)}, u32[]{:S(2)}) async-start(f32[16,8,128]{2,1,0:T(8,128)} %middle_send.1.after), calls=%async_computation.1 | async-start | bytes 131072 | tf_op jit(solution)/shard_map/all_to_all | solution.py:363
  51.3 51.0 %copy-start = (f32[32,512]{1,0:T(8,128)S(1)}, f32[32,512]{1,0:T(8,128)}, u32[]{:S(2)}) copy-start(f32[32,512]{1,0:T(8,128)} %direction.1) | copy-start | bytes 196612
  51.3 51.0 %copy-start.1 = (f32[32,512]{1,0:T(8,128)S(1)}, f32[32,512]{1,0:T(8,128)}, u32[]{:S(2)}) copy-start(f32[32,512]{1,0:T(8,128)} %residual.1) | copy-start | bytes 196612
  51.3 51.0 %copy-start.2 = (f32[32,512]{1,0:T(8,128)S(1)}, f32[32,512]{1,0:T(8,128)}, u32[]{:S(2)}) copy-start(f32[32,512]{1,0:T(8,128)} %solution.1) | copy-start | bytes 196612
  52.1 14.3 %all-to-all-start.2 = ((f32[32,16,128]{2,1,0:T(8,128)}), f32[32,16,128]{2,1,0:T(8,128)S(1)}, u32[]{:S(2)}, u32[]{:S(2)}) async-start(f32[32,16,128]{2,1,0:T(8,128)} %middle_return.1.after), calls=%async_computation.2 | async-start | bytes 524288 | tf_op jit(solution)/shard_map/all_to_all | solution.py:363
  56.2 8.9 %collective-permute-start = (f32[32,256]{1,0:T(8,128)S(1)}, f32[32,256]{1,0:T(8,128)S(1)}, u32[]{:S(2)}, u32[]{:S(2)}) collective-permute-start(f32[32,256]{1,0:T(8,128)S(1)} %get-tuple-element.16.own_first), channel_id=1, source_target_pairs={{0,1},{1,0},{2,3},{3,2},{4,5},{5,4},{6,7},{7,6},{8,9},{9,8},{10,11... | collective-permute-start | bytes 98312 | tf_op jit(solution)/shard_map/ppermute | solution.py:391

commit v2 on v1

--- a/solution.py
+++ b/solution.py
@@ -21,27 +21,27 @@
 highest = lax.Precision.HIGHEST
 
 
+COSINE_DEGREE = 6
+
+
 def cosine_coefficients():
     cheb = np.polynomial.chebyshev
     nodes = np.cos(np.pi * (np.arange(64) + 0.5) / 64)
-    squares = np.pi**2 * (nodes + 1.0) / 2.0
-    series = cheb.chebfit(nodes, np.cos(np.sqrt(squares)), 7)
+    series = cheb.chebfit(nodes, np.cos(2.0 * np.pi * np.sqrt((nodes + 1.0) / 8.0)), COSINE_DEGREE)
     poly = np.polynomial.Polynomial(cheb.cheb2poly(series))
-    shifted = poly(np.polynomial.Polynomial([-1.0, 2.0 / np.pi**2]))
+    shifted = poly(np.polynomial.Polynomial([-1.0, 8.0]))
     return [float(value) for value in shifted.coef * math.sqrt(2.0 / RANK)]
 
 
 COSINE = cosine_coefficients()
-TURN_HIGH = 6.28125
-TURN_LOW = 2.0 * math.pi - TURN_HIGH
-
-
-def scaled_cosine(angle):
-    turns = jnp.round(angle * (1.0 / (2.0 * math.pi)))
-    reduced = (angle - turns * TURN_HIGH) - turns * TURN_LOW
-    square = reduced * reduced
-    value = jnp.full_like(square, COSINE[-1])
-    for coefficient in COSINE[-2::-1]:
+TURN = 2.0 * math.pi
+
+
+def scaled_cosine(turns):
+    part = turns - jnp.round(turns)
+    square = part * part
+    value = COSINE[-1] * square + COSINE[-2]
+    for coefficient in COSINE[-3::-1]:
         value = value * square + coefficient
     return value
 
@@ -104,13 +104,14 @@
     for load in loads:
         load.wait()
     proj[...] = mm(emb[...], freq[...])
+    phase_turns = phase[...] * (1.0 / TURN)
 
     def chunk(step, carry):
         rows = pl.ds(pl.multiple_of(step * CHUNK, CHUNK), CHUNK)
         block = proj[rows, :]
         for level in range(LEVELS):
-            angle = block * (1.0 / length_scale(level + 1)) + phase[level : level + 1, :]
-            value = scaled_cosine(angle)
+            turns = block * (1.0 / (TURN * length_scale(level + 1))) + phase_turns[level : level + 1, :]
+            value = scaled_cosine(turns)
             keep[level, rows, :] = value
             high_part, low_part = split(value)
             high[level, rows, :] = high_part
@@ -157,22 +158,17 @@
             error = gain * mm3(error_parts, error_parts) - (gain / double) * eye
             scale = jnp.minimum(double - 1.0, 1e4)
     block_parts = split(block)
-    for step in range(3):
-        if step < 2:
+    for step in range(2):
+        if step < 1:
             error = eye - mm3(block_parts, split(inverse))
         else:
             error = eye - mm6(block, inverse)
-        inverse_high, inverse_low = split(inverse)
-        if step < 1:
-            inverse = inverse + mm3((inverse_high, inverse_low), split(error))
-        else:
-            inverse = inverse + mm(inverse_high, error.astype(bf16))
+        inverse = inverse + mm3(split(inverse), split(error))
     return inverse
 
 
-def leaf_first_kernel(
-    emb_in, direction_in, after, near, first_out, across_out, schur_out, largest_out,
-    emb, direction, grid, matrix, sems,
+def leaf_matrix_kernel(
+    emb_in, direction_in, after, near, matrix, largest_out, emb, direction, grid, sems
 ):
     loads = [
         pltpu.make_async_copy(emb_in, emb, sems.at[0]),
@@ -207,32 +203,43 @@
     sums = jnp.sum(matrix[...], axis=0, keepdims=True)
     largest = jnp.max(sums, axis=1, keepdims=True)
     largest_out[...] = jnp.broadcast_to(largest, (8, 128))
+
+
+def leaf_first_kernel(matrix, largest, after, first_out, across_out, schur_out):
     side = matrix[:HALF, HALF:]
-    first = inverse_block(matrix[:HALF, :HALF], largest)
+    first = inverse_block(matrix[:HALF, :HALF], largest[:1, :1])
     across = mm6(first, side)
     first_out[...] = first
     across_out[...] = across
     schur_out[...] = matrix[HALF:, HALF:] - mm6(jnp.transpose(across), side)
 
 
-def leaf_second_kernel(first, across_in, schur, largest, residual_in, after, solved, inv, residual, sem):
+def leaf_second_kernel(
+    first, across_in, schur, largest, matrix, residual_in, after, solved, inv, residual, whole_inverse, sem
+):
     load = pltpu.make_async_copy(residual_in, residual, sem.at[0])
     load.start()
     across = across_in[...]
     second = inverse_block(schur[...], largest[:1, :1])
     lower = -mm6(second, jnp.transpose(across))
     top = first[...] - mm6(across, lower)
-    left = jnp.concatenate([top, lower], axis=0)
-    right = jnp.concatenate([jnp.transpose(lower), second], axis=0)
-    for n, plane in enumerate(planes(left)):
-        inv[n, :, :HALF] = plane
-    for n, plane in enumerate(planes(right)):
-        inv[n, :, HALF:] = plane
+    whole_inverse[:HALF, :HALF] = top
+    whole_inverse[HALF:, :HALF] = lower
+    whole_inverse[:HALF, HALF:] = jnp.transpose(lower)
+    whole_inverse[HALF:, HALF:] = second
+    row = lax.broadcasted_iota(jnp.int32, (LEAF, LEAF), 0)
+    column = lax.broadcasted_iota(jnp.int32, (LEAF, LEAF), 1)
+    start = whole_inverse[...]
+    start_planes = planes(start)
+    error = jnp.where(row == column, 1.0, 0.0) - six_products(planes(matrix[...]), start_planes, mm)
+    better = start + mm3(start_planes[:2], split(error))
+    for n, plane in enumerate(planes(better)):
+        inv[n] = plane
     load.wait()
     solved[...] = six_products(planes(residual[...]), [inv[n] for n in range(3)], mm)
 
 
-def middle_send_kernel(received, out):
+def middle_send_kernel(received, first_after, second_after, out):
     total = received[0, 8:16, :]
     for source in range(1, PTS):
         total = total + received[source, 8:16, :]
@@ -390,26 +397,30 @@
     )
     other_first = lax.ppermute(part_first, "z", [(n, n ^ 1) for n in range(8)])
     received = exchange(part.reshape(ROWS, 16, 128), ("x", "z"))
-    middle = call(middle_send_kernel, whole((GRP, 8, 128)), received, name="middle_send")
+    near, matrix, largest = call(
+        leaf_matrix_kernel, (rows, whole((LEAF, LEAF)), whole((8, 128))), embeddings, direction, part_first,
+        hbm=[(0, "hbm"), (1, "hbm"), (2, "any")],
+        scratch=(leaf_points, leaf_rows, pltpu.VMEM((LEAF, LEAF), f32), pltpu.SemaphoreType.DMA((2,))),
+        name="leaf_matrix",
+    )
+    middle = call(
+        middle_send_kernel, whole((GRP, 8, 128)), received, largest, other_first,
+        hbm=[(1, "any"), (2, "any")], name="middle_send",
+    )
     wide = exchange(middle, ("y", "c"))
-    near, first, across, schur, largest = call(
-        leaf_first_kernel, (rows, half, half, half, whole((8, 128))), embeddings, direction, middle,
-        hbm=[(0, "hbm"), (1, "hbm"), (2, "any")],
-        scratch=(
-            leaf_points, leaf_rows, pltpu.VMEM((LEAF, LEAF), f32), pltpu.VMEM((LEAF, LEAF), f32),
-            pltpu.SemaphoreType.DMA((2,)),
-        ),
-        name="leaf_first",
+    first, across, schur = call(
+        leaf_first_kernel, (half, half, half), matrix, largest, middle, hbm=[(2, "any")], name="leaf_first"
     )
     place = lax.axis_index("y").astype(jnp.int32).reshape(1)
     back = call(
-        middle_return_kernel, whole((PTS, 16, 128)), place, received, wide, largest,
+        middle_return_kernel, whole((PTS, 16, 128)), place, received, wide, schur,
         hbm=[(3, "any")], scalars=1, name="middle_return",
     )
     returned = exchange(back, ("x", "z"))
     solved, inv = call(
-        leaf_second_kernel, (rows, whole((3, LEAF, LEAF), bf16)), first, across, schur, largest, residual, back,
-        hbm=[(4, "hbm"), (5, "any")], scratch=(leaf_rows, pltpu.SemaphoreType.DMA((1,))), name="leaf_second",
+        leaf_second_kernel, (rows, whole((3, LEAF, LEAF), bf16)), first, across, schur, largest, matrix, residual, back,
+        hbm=[(5, "hbm"), (6, "any")],
+        scratch=(leaf_rows, pltpu.VMEM((LEAF, LEAF), f32), pltpu.SemaphoreType.DMA((1,))), name="leaf_second",
     )
     image, shifted, sums = call(
         image_kernel, (rows, rows, whole((1, 128))),

time: 104 us -> 103 us (level)
  blocking collectives: 55.1 us -> 31.7 us
  starting transfers between devices: 18.3 us -> 32.5 us
  local copies, waits for them, and re-layouts: 0.03 us -> 3.35 us
  waiting for transfers between devices: 1.23 us -> 4.48 us
  Pallas kernels: 27.8 us -> 29.7 us
    all_to_all x3 -> x2, blocking collectives: 55.1 us -> 31.7 us  [exchange(): return lax.all_to_all(value, axes, 0, 0, tiled=True)]
    all_to_all x2 -> x3, starting transfers between devices: 15 us -> 29.4 us  [exchange(): return lax.all_to_all(value, axes, 0, 0, tiled=True)]
    unnamed x6 -> x14, local copies, waits for them, and re-layouts: 0.02 us -> 3.34 us
    all_to_all x2 -> x3, waiting for transfers between devices: 1.23 us -> 3.93 us  [exchange(): return lax.all_to_all(value, axes, 0, 0, tiled=True)]
    pallas_call x8 -> x9, Pallas kernels: 27.8 us -> 29.7 us  [call(): pl.pallas_call(kernel, out_shape=outs, in_specs=specs, out_specs=vmem if...]
  transfers between devices with their start and end apart: 3 -> 4, of which waited for: 1 -> 4; matrix products, arithmetic and copies ran while one was open for 0% -> 0% of each run, Pallas kernels for 14% -> 16%
where the time goes in v2:
time: 103 us
  starting transfers between devices  32.5 us (32%)
  blocking collectives  31.7 us (31%)
  Pallas kernels  29.7 us (29%)
  waiting for transfers between devices  4.48 us (4%)
  local copies, waits for them, and re-layouts  3.35 us (3%)
    all_to_all x2, blocking collectives, exchange(): return lax.all_to_all(value, axes, 0, 0, tiled=True)  31.7 us
    pallas_call x9, Pallas kernels, call(): pl.pallas_call(kernel, out_shape=outs, in_specs=specs, out_specs=vmem if...  29.7 us
    all_to_all x3, starting transfers between devices, exchange(): return lax.all_to_all(value, axes, 0, 0, tiled=True)  29.4 us
    all_to_all x3, waiting for transfers between devices, exchange(): return lax.all_to_all(value, axes, 0, 0, tiled=True)  3.93 us
    unnamed x14, local copies, waits for them, and re-layouts  3.34 us
    ppermute x1, starting transfers between devices, body(): other_first = lax.ppermute(part_first, 'z', [(n, n ^ 1) for n in range(8)])  3.14 us
  transfers between devices with their start and end apart: 4, of which 4 were waited for; matrix products, arithmetic and copies ran while one was open for 0% of the time, Pallas kernels for 16%

profile of v2, /device:TPU:1, one launch (start us, length us, event | category | flops | bytes accessed | tf_op | source)
XLA Modules:
  0.0 102.5 jit_solution(7502502001483677137)
XLA Ops:
  0.6 7.1 %features.1 = (f32[9,512,256]{2,1,0:T(8,128)}, f32[32,256]{1,0:T(8,128)S(1)}, f32[512,128]{1,0:T(8,128)}) custom-call(bf16[512,768]{1,0:T(8,128)(2,1)} %emb_in.3, bf16[768,256]{1,0:T(8,128)(2,1)} %freq_in.1, f32[9,256]{1,0:T(8,128)} %phase_in.1, f32[32,512]{1,0:T(8,128)} %direction.1), custom_call_target="tpu_custom_call" | custom-call | tf_op jit(solution)/shard_map/features/pallas_call | solution.py:358
  7.7 13.7 %all-to-all-start = ((f32[32,16,128]{2,1,0:T(8,128)}), f32[32,16,128]{2,1,0:T(8,128)S(1)}, u32[]{:S(2)}, u32[]{:S(2)}) async-start(f32[32,16,128]{2,1,0:T(8,128)} %bitcast.1), calls=%async_computation | async-start | bytes 524288 | tf_op jit(solution)/shard_map/all_to_all | solution.py:370
  21.4 3.1 %collective-permute-start = (f32[32,256]{1,0:T(8,128)S(1)}, f32[32,256]{1,0:T(8,128)S(1)}, u32[]{:S(2)}, u32[]{:S(2)}) collective-permute-start(f32[32,256]{1,0:T(8,128)S(1)} %get-tuple-element.17.after.own_first), channel_id=1, source_target_pairs={{0,1},{1,0},{2,3},{3,2},{4,5},{5,4},{6,7},{7,6},{8,9},{9,8},{10,11... | collective-permute-start | bytes 98312 | tf_op jit(solution)/shard_map/ppermute | solution.py:398
  24.6 3.9 %leaf_matrix.1 = (f32[32,512]{1,0:T(8,128)S(1)}, f32[512,512]{1,0:T(8,128)S(1)}, f32[8,128]{1,0:T(8,128)S(1)}) custom-call(bf16[512,768]{1,0:T(8,128)(2,1)} %emb_in.3, f32[32,512]{1,0:T(8,128)} %direction.1, f32[32,256]{1,0:T(8,128)S(1)} %get-tuple-element.17.after.own_first), custom_call_target="tpu_custom_call" | custom-call | tf_op jit(solution)/shard_map/leaf_matrix/pallas_call | solution.py:358
  28.5 0.6 collective-permute-done.second_after.other_first
  29.0 2.1 %all-to-all-done.received = f32[32,16,128]{2,1,0:T(8,128)S(1)} async-done(((f32[32,16,128]{2,1,0:T(8,128)}), f32[32,16,128]{2,1,0:T(8,128)S(1)}, u32[]{:S(2)}, u32[]{:S(2)}) %all-to-all-start) | async-done | bytes 262176 | tf_op jit(solution)/shard_map/all_to_all | solution.py:370
  31.1 0.7 middle_send.1.after
  31.8 11.1 %all-to-all-start.1 = ((f32[16,8,128]{2,1,0:T(8,128)}), f32[16,8,128]{2,1,0:T(8,128)S(1)}, u32[]{:S(2)}, u32[]{:S(2)}) async-start(f32[16,8,128]{2,1,0:T(8,128)} %middle_send.1.after), calls=%async_computation.1 | async-start | bytes 131072 | tf_op jit(solution)/shard_map/all_to_all | solution.py:370
  42.9 4.6 %leaf_first.1 = (f32[256,256]{1,0:T(8,128)S(1)}, f32[256,256]{1,0:T(8,128)S(1)}, f32[256,256]{1,0:T(8,128)S(1)}) custom-call(f32[512,512]{1,0:T(8,128)S(1)} %get-tuple-element.20.matrix, f32[8,128]{1,0:T(8,128)S(1)} %get-tuple-element.19.first_after.largest, f32[16,8,128]{2,1,0:T(8,128)} %middle_send.1.after), custom_call_target="tpu_custom_call" | custom-call | tf_op jit(solution)/shard_map/leaf_first/pallas_call | solution.py:358
  47.5 0.0 copy-start.2
  47.5 0.7 copy-done.2
  48.2 0.7 copy-done.4
  49.0 1.7 %all-to-all-done.1.wide = f32[16,8,128]{2,1,0:T(8,128)S(1)} async-done(((f32[16,8,128]{2,1,0:T(8,128)}), f32[16,8,128]{2,1,0:T(8,128)S(1)}, u32[]{:S(2)}, u32[]{:S(2)}) %all-to-all-start.1) | async-done | bytes 65568 | tf_op jit(solution)/shard_map/all_to_all | solution.py:370
  50.7 0.7 middle_return.1.after
  51.4 4.5 %all-to-all-start.2 = ((f32[32,16,128]{2,1,0:T(8,128)}), f32[32,16,128]{2,1,0:T(8,128)S(1)}, u32[]{:S(2)}, u32[]{:S(2)}) async-start(f32[32,16,128]{2,1,0:T(8,128)} %middle_return.1.after), calls=%async_computation.2 | async-start | bytes 524288 | tf_op jit(solution)/shard_map/all_to_all | solution.py:370
  55.9 0.0 copy-start.3
  56.0 0.9 copy-done.3
  56.9 0.9 copy-done.5
  57.9 7.9 %leaf_second.1 = (f32[32,512]{1,0:T(8,128)S(1)}, bf16[3,512,512]{2,1,0:T(8,128)(2,1)S(1)}) custom-call(f32[256,256]{1,0:T(8,128)S(1)} %copy-done.3, f32[256,256]{1,0:T(8,128)S(1)} %copy-done.5, f32[256,256]{1,0:T(8,128)S(1)} %get-tuple-element.21.after.schur, f32[8,128]{1,0:T(8,128)S(1)} %get-tuple-element.19.first_after.largest, ...), custom_call_target="tpu_custom_call" | custom-call | tf_op jit(solution)/shard_map/leaf_second/pallas_call | solution.py:358
  65.8 0.1 all-to-all-done.2
  65.9 4.0 %image.1 = (f32[32,512]{1,0:T(8,128)S(1)}, f32[32,512]{1,0:T(8,128)S(1)}, f32[1,128]{1,0:T(1,128)S(1)}) custom-call(f32[32,256]{1,0:T(8,128)S(1)} %get-tuple-element.17.after.own_first, f32[32,256]{1,0:T(8,128)S(1)} %collective-permute-done.second_after.other_first, f32[512,128]{1,0:T(8,128)S(1)} %bitcast.4, f32[9,512,256]{2,1,0:T(8,128)} %get-tuple-element.22.feat_in, ...), custom_call_target="tpu_custom_call" | custom-call | tf_op jit(solution)/shard_map/image/pallas_call | solution.py:358
  69.9 17.4 %all_to_all.25.received = f32[32,1,128]{2,1,0:T(1,128)S(1)} all-to-all(f32[32,1,128]{2,1,0:T(1,128)S(1)} %broadcast_in_dim.9), channel_id=1, replica_groups=mesh['y'=8,'c'=2,'x'=4,'z'=8] {'x','z'}, dimensions={0} | all-to-all | bytes 32768 | tf_op jit(solution)/shard_map/all_to_all | solution.py:370
  87.4 14.3 %all_to_all.26.received = f32[16,1,128]{2,1,0:T(1,128)S(1)} all-to-all(f32[16,1,128]{2,1,0:T(1,128)S(1)} %sum_spread.1), channel_id=1, replica_groups=mesh['y'=8,'c'=2,'x'=4,'z'=8] {'y','c'}, dimensions={0} | all-to-all | bytes 16384 | tf_op jit(solution)/shard_map/all_to_all | solution.py:370
  101.7 0.8 finish.1
  (10 shorter events, 0.1 us)
Async XLA Ops:
  7.7 23.4 %all-to-all-start = ((f32[32,16,128]{2,1,0:T(8,128)}), f32[32,16,128]{2,1,0:T(8,128)S(1)}, u32[]{:S(2)}, u32[]{:S(2)}) async-start(f32[32,16,128]{2,1,0:T(8,128)} %bitcast.1), calls=%async_computation | async-start | bytes 524288 | tf_op jit(solution)/shard_map/all_to_all | solution.py:370
  21.4 7.6 %collective-permute-start = (f32[32,256]{1,0:T(8,128)S(1)}, f32[32,256]{1,0:T(8,128)S(1)}, u32[]{:S(2)}, u32[]{:S(2)}) collective-permute-start(f32[32,256]{1,0:T(8,128)S(1)} %get-tuple-element.17.after.own_first), channel_id=1, source_target_pairs={{0,1},{1,0},{2,3},{3,2},{4,5},{5,4},{6,7},{7,6},{8,9},{9,8},{10,11... | collective-permute-start | bytes 98312 | tf_op jit(solution)/shard_map/ppermute | solution.py:398
  31.8 18.9 %all-to-all-start.1 = ((f32[16,8,128]{2,1,0:T(8,128)}), f32[16,8,128]{2,1,0:T(8,128)S(1)}, u32[]{:S(2)}, u32[]{:S(2)}) async-start(f32[16,8,128]{2,1,0:T(8,128)} %middle_send.1.after), calls=%async_computation.1 | async-start | bytes 131072 | tf_op jit(solution)/shard_map/all_to_all | solution.py:370
  47.5 0.7 copy-start.2
  48.2 0.7 copy-start.4
  51.4 50.3 %copy-start = (f32[32,512]{1,0:T(8,128)S(1)}, f32[32,512]{1,0:T(8,128)}, u32[]{:S(2)}) copy-start(f32[32,512]{1,0:T(8,128)} %direction.1) | copy-start | bytes 196612
  51.4 50.3 %copy-start.1 = (f32[32,512]{1,0:T(8,128)S(1)}, f32[32,512]{1,0:T(8,128)}, u32[]{:S(2)}) copy-start(f32[32,512]{1,0:T(8,128)} %residual.1) | copy-start | bytes 196612
  51.4 50.3 %copy-start.6 = (f32[32,512]{1,0:T(8,128)S(1)}, f32[32,512]{1,0:T(8,128)}, u32[]{:S(2)}) copy-start(f32[32,512]{1,0:T(8,128)} %solution.1) | copy-start | bytes 196612
  51.4 14.5 %all-to-all-start.2 = ((f32[32,16,128]{2,1,0:T(8,128)}), f32[32,16,128]{2,1,0:T(8,128)S(1)}, u32[]{:S(2)}, u32[]{:S(2)}) async-start(f32[32,16,128]{2,1,0:T(8,128)} %middle_return.1.after), calls=%async_computation.2 | async-start | bytes 524288 | tf_op jit(solution)/shard_map/all_to_all | solution.py:370
  55.9 1.0 copy-start.3
  56.9 0.9 copy-start.5

commit v3 on v2

--- a/solution.py
+++ b/solution.py
@@ -146,7 +146,7 @@
     scale = jnp.minimum((largest + RIDGE) / jnp.maximum(largest - RIDGE, 1e-3), 1e4)
     error = eye - start * block
     inverse = None
-    for step in range(6):
+    for step in range(7):
         double = 2.0 * scale * scale
         gain = double / (double - 1.0)
         error_parts = split(error)
@@ -154,16 +154,11 @@
             inverse = (gain * start) * (eye + error)
         else:
             inverse = gain * (inverse + mm3(split(inverse), error_parts))
-        if step < 5:
+        if step < 6:
             error = gain * mm3(error_parts, error_parts) - (gain / double) * eye
             scale = jnp.minimum(double - 1.0, 1e4)
-    block_parts = split(block)
-    for step in range(2):
-        if step < 1:
-            error = eye - mm3(block_parts, split(inverse))
-        else:
-            error = eye - mm6(block, inverse)
-        inverse = inverse + mm3(split(inverse), split(error))
+    error = eye - mm6(block, inverse)
+    inverse = inverse + mm3(split(inverse), split(error))
     return inverse
 
 
@@ -205,22 +200,39 @@
     largest_out[...] = jnp.broadcast_to(largest, (8, 128))
 
 
-def leaf_first_kernel(matrix, largest, after, first_out, across_out, schur_out):
+def leaf_first_kernel(matrix, largest, after, first_out, across_out, schur_out, first_keep, across_keep, sems):
     side = matrix[:HALF, HALF:]
     first = inverse_block(matrix[:HALF, :HALF], largest[:1, :1])
+    first_keep[...] = first
     across = mm6(first, side)
-    first_out[...] = first
-    across_out[...] = across
+    across_keep[...] = across
+    stores = [
+        pltpu.make_async_copy(first_keep, first_out, sems.at[0]),
+        pltpu.make_async_copy(across_keep, across_out, sems.at[1]),
+    ]
+    for store in stores:
+        store.start()
     schur_out[...] = matrix[HALF:, HALF:] - mm6(jnp.transpose(across), side)
+    for store in stores:
+        store.wait()
 
 
 def leaf_second_kernel(
-    first, across_in, schur, largest, matrix, residual_in, after, solved, inv, residual, whole_inverse, sem
+    first_in, across_in, schur, largest, matrix, residual_in, after, solved, inv,
+    first, across_scratch, residual, whole_inverse, sems,
 ):
-    load = pltpu.make_async_copy(residual_in, residual, sem.at[0])
-    load.start()
-    across = across_in[...]
+    loads = [
+        pltpu.make_async_copy(source, target, sems.at[n])
+        for n, (source, target) in enumerate(
+            ((first_in, first), (across_in, across_scratch), (residual_in, residual))
+        )
+    ]
+    for load in loads:
+        load.start()
     second = inverse_block(schur[...], largest[:1, :1])
+    for load in loads:
+        load.wait()
+    across = across_scratch[...]
     lower = -mm6(second, jnp.transpose(across))
     top = first[...] - mm6(across, lower)
     whole_inverse[:HALF, :HALF] = top
@@ -232,10 +244,10 @@
     start = whole_inverse[...]
     start_planes = planes(start)
     error = jnp.where(row == column, 1.0, 0.0) - six_products(planes(matrix[...]), start_planes, mm)
-    better = start + mm3(start_planes[:2], split(error))
+    error_high = error.astype(bf16)
+    better = start + (mm(start_planes[0], error_high) + mm(start_planes[1], error_high))
     for n, plane in enumerate(planes(better)):
         inv[n] = plane
-    load.wait()
     solved[...] = six_products(planes(residual[...]), [inv[n] for n in range(3)], mm)
 
 
@@ -357,7 +369,9 @@
             args[place] = pltpu.with_memory_space_constraint(args[place], pltpu.HBM)
     return pl.pallas_call(
         kernel,
-        out_shape=outs,
+        out_shape=outs if single else tuple(
+            pltpu.HBM(out.shape, out.dtype) if n in hbm_out else out for n, out in enumerate(outs)
+        ),
         in_specs=specs,
         out_specs=vmem if single else tuple(far if n in hbm_out else vmem for n in range(len(outs))),
         scratch_shapes=list(scratch),
@@ -375,6 +389,7 @@
     half = whole((HALF, HALF))
     leaf_points = pltpu.VMEM((LEAF, EMBED), bf16)
     leaf_rows = pltpu.VMEM((ROWS, LEAF), f32)
+    block = pltpu.VMEM((HALF, HALF), f32)
     panel = pltpu.VMEM((LEVELS, LEAF, RANK), f32)
     feat, part_first, part = call(
         features_kernel,
@@ -409,7 +424,8 @@
     )
     wide = exchange(middle, ("y", "c"))
     first, across, schur = call(
-        leaf_first_kernel, (half, half, half), matrix, largest, middle, hbm=[(2, "any")], name="leaf_first"
+        leaf_first_kernel, (half, half, half), matrix, largest, middle, hbm=[(2, "any")], hbm_out=(0, 1),
+        scratch=(block, block, pltpu.SemaphoreType.DMA((2,))), name="leaf_first",
     )
     place = lax.axis_index("y").astype(jnp.int32).reshape(1)
     back = call(
@@ -419,8 +435,9 @@
     returned = exchange(back, ("x", "z"))
     solved, inv = call(
         leaf_second_kernel, (rows, whole((3, LEAF, LEAF), bf16)), first, across, schur, largest, matrix, residual, back,
-        hbm=[(5, "hbm"), (6, "any")],
-        scratch=(leaf_rows, pltpu.VMEM((LEAF, LEAF), f32), pltpu.SemaphoreType.DMA((1,))), name="leaf_second",
+        hbm=[(0, "hbm"), (1, "hbm"), (5, "hbm"), (6, "any")],
+        scratch=(block, block, leaf_rows, pltpu.VMEM((LEAF, LEAF), f32), pltpu.SemaphoreType.DMA((3,))),
+        name="leaf_second",
     )
     image, shifted, sums = call(
         image_kernel, (rows, rows, whole((1, 128))),

time: 103 us -> 99.4 us (0.965)
  waiting for transfers between devices: 4.48 us -> 8.2 us
  blocking collectives: 31.7 us -> 28 us
  local copies, waits for them, and re-layouts: 3.35 us -> 0.02 us
    all_to_all x3, waiting for transfers between devices: 3.93 us -> 7.64 us  [exchange(): return lax.all_to_all(value, axes, 0, 0, tiled=True)]
    all_to_all x2, blocking collectives: 31.7 us -> 28 us  [exchange(): return lax.all_to_all(value, axes, 0, 0, tiled=True)]
    unnamed x14 -> x6, local copies, waits for them, and re-layouts: 3.34 us -> 0.01 us
where the time goes in v3:
time: 99.4 us; the launch traced here: 98.8 us
  starting transfers between devices  32.5 us (33%)
  Pallas kernels  29.4 us (30%)
  blocking collectives  28 us (28%)
  waiting for transfers between devices  8.2 us (8%)
    pallas_call x9, Pallas kernels, call(): pl.pallas_call(kernel, out_shape=outs if single else tuple((pltpu.HBM(out...  29.4 us
    all_to_all x3, starting transfers between devices, exchange(): return lax.all_to_all(value, axes, 0, 0, tiled=True)  29.4 us
    all_to_all x2, blocking collectives, exchange(): return lax.all_to_all(value, axes, 0, 0, tiled=True)  28 us
    all_to_all x3, waiting for transfers between devices, exchange(): return lax.all_to_all(value, axes, 0, 0, tiled=True)  7.64 us
    ppermute x1, starting transfers between devices, body(): other_first = lax.ppermute(part_first, 'z', [(n, n ^ 1) for n in range(8)])  3.14 us
  transfers between devices with their start and end apart: 4, of which 4 were waited for; matrix products, arithmetic and copies ran while one was open for 0% of the time, Pallas kernels for 16%

profile of v3, /device:TPU:1, one launch (start us, length us, event | category | flops | bytes accessed | tf_op | source)
XLA Modules:
  0.0 98.8 jit_solution(676711061148194798)
XLA Ops:
  0.6 7.1 %features.1 = (f32[9,512,256]{2,1,0:T(8,128)}, f32[32,256]{1,0:T(8,128)S(1)}, f32[512,128]{1,0:T(8,128)}) custom-call(bf16[512,768]{1,0:T(8,128)(2,1)} %emb_in.3, bf16[768,256]{1,0:T(8,128)(2,1)} %freq_in.1, f32[9,256]{1,0:T(8,128)} %phase_in.1, f32[32,512]{1,0:T(8,128)} %direction.1), custom_call_target="tpu_custom_call" | custom-call | tf_op jit(solution)/shard_map/features/pallas_call | solution.py:370
  7.7 13.7 %all-to-all-start = ((f32[32,16,128]{2,1,0:T(8,128)}), f32[32,16,128]{2,1,0:T(8,128)S(1)}, u32[]{:S(2)}, u32[]{:S(2)}) async-start(f32[32,16,128]{2,1,0:T(8,128)} %bitcast.1), calls=%async_computation | async-start | bytes 524288 | tf_op jit(solution)/shard_map/all_to_all | solution.py:384
  21.5 3.1 %collective-permute-start = (f32[32,256]{1,0:T(8,128)S(1)}, f32[32,256]{1,0:T(8,128)S(1)}, u32[]{:S(2)}, u32[]{:S(2)}) collective-permute-start(f32[32,256]{1,0:T(8,128)S(1)} %get-tuple-element.17.after.own_first), channel_id=1, source_target_pairs={{0,1},{1,0},{2,3},{3,2},{4,5},{5,4},{6,7},{7,6},{8,9},{9,8},{10,11... | collective-permute-start | bytes 98312 | tf_op jit(solution)/shard_map/ppermute | solution.py:413
  24.6 3.9 %leaf_matrix.1 = (f32[32,512]{1,0:T(8,128)S(1)}, f32[512,512]{1,0:T(8,128)S(1)}, f32[8,128]{1,0:T(8,128)S(1)}) custom-call(bf16[512,768]{1,0:T(8,128)(2,1)} %emb_in.3, f32[32,512]{1,0:T(8,128)} %direction.1, f32[32,256]{1,0:T(8,128)S(1)} %get-tuple-element.17.after.own_first), custom_call_target="tpu_custom_call" | custom-call | tf_op jit(solution)/shard_map/leaf_matrix/pallas_call | solution.py:370
  28.5 0.6 collective-permute-done.second_after.other_first
  29.0 2.1 %all-to-all-done.received = f32[32,16,128]{2,1,0:T(8,128)S(1)} async-done(((f32[32,16,128]{2,1,0:T(8,128)}), f32[32,16,128]{2,1,0:T(8,128)S(1)}, u32[]{:S(2)}, u32[]{:S(2)}) %all-to-all-start) | async-done | bytes 262176 | tf_op jit(solution)/shard_map/all_to_all | solution.py:384
  31.1 0.7 middle_send.1.after
  31.8 11.1 %all-to-all-start.1 = ((f32[16,8,128]{2,1,0:T(8,128)}), f32[16,8,128]{2,1,0:T(8,128)S(1)}, u32[]{:S(2)}, u32[]{:S(2)}) async-start(f32[16,8,128]{2,1,0:T(8,128)} %middle_send.1.after), calls=%async_computation.1 | async-start | bytes 131072 | tf_op jit(solution)/shard_map/all_to_all | solution.py:384
  42.9 4.5 %leaf_first.1 = (f32[256,256]{1,0:T(8,128)}, f32[256,256]{1,0:T(8,128)}, f32[256,256]{1,0:T(8,128)S(1)}) custom-call(f32[512,512]{1,0:T(8,128)S(1)} %get-tuple-element.20.matrix, f32[8,128]{1,0:T(8,128)S(1)} %get-tuple-element.19.first_after.largest, f32[16,8,128]{2,1,0:T(8,128)} %middle_send.1.after), custom_call_target="tpu_custom_call" | custom-call | tf_op jit(solution)/shard_map/leaf_first/pallas_call | solution.py:370
  47.4 3.3 %all-to-all-done.1.wide = f32[16,8,128]{2,1,0:T(8,128)S(1)} async-done(((f32[16,8,128]{2,1,0:T(8,128)}), f32[16,8,128]{2,1,0:T(8,128)S(1)}, u32[]{:S(2)}, u32[]{:S(2)}) %all-to-all-start.1) | async-done | bytes 65568 | tf_op jit(solution)/shard_map/all_to_all | solution.py:384
  50.7 0.8 middle_return.1.after
  51.5 0.0 copy-start
  51.5 0.0 copy-start.1
  51.5 0.0 copy-start.2
  51.5 4.5 %all-to-all-start.2 = ((f32[32,16,128]{2,1,0:T(8,128)}), f32[32,16,128]{2,1,0:T(8,128)S(1)}, u32[]{:S(2)}, u32[]{:S(2)}) async-start(f32[32,16,128]{2,1,0:T(8,128)} %middle_return.1.after), calls=%async_computation.2 | async-start | bytes 524288 | tf_op jit(solution)/shard_map/all_to_all | solution.py:384
  56.0 7.7 %leaf_second.1 = (f32[32,512]{1,0:T(8,128)S(1)}, bf16[3,512,512]{2,1,0:T(8,128)(2,1)S(1)}) custom-call(f32[256,256]{1,0:T(8,128)} %get-tuple-element.24.first_in, f32[256,256]{1,0:T(8,128)} %get-tuple-element.25.across_in, f32[256,256]{1,0:T(8,128)S(1)} %get-tuple-element.21.after.schur, f32[8,128]{1,0:T(8,128)S(1)} %get-tuple-element.19.first_after.largest, ...), custom_call_target="tpu_custom_call" | custom-call | tf_op jit(solution)/shard_map/leaf_second/pallas_call | solution.py:370
  63.6 2.3 %all-to-all-done.2 = f32[32,16,128]{2,1,0:T(8,128)S(1)} async-done(((f32[32,16,128]{2,1,0:T(8,128)}), f32[32,16,128]{2,1,0:T(8,128)S(1)}, u32[]{:S(2)}, u32[]{:S(2)}) %all-to-all-start.2) | async-done | bytes 262176 | tf_op jit(solution)/shard_map/all_to_all | solution.py:384
  65.9 4.0 %image.1 = (f32[32,512]{1,0:T(8,128)S(1)}, f32[32,512]{1,0:T(8,128)S(1)}, f32[1,128]{1,0:T(1,128)S(1)}) custom-call(f32[32,256]{1,0:T(8,128)S(1)} %get-tuple-element.17.after.own_first, f32[32,256]{1,0:T(8,128)S(1)} %collective-permute-done.second_after.other_first, f32[512,128]{1,0:T(8,128)S(1)} %bitcast.4, f32[9,512,256]{2,1,0:T(8,128)} %get-tuple-element.22.feat_in, ...), custom_call_target="tpu_custom_call" | custom-call | tf_op jit(solution)/shard_map/image/pallas_call | solution.py:370
  70.0 15.2 %all_to_all.25.received = f32[32,1,128]{2,1,0:T(1,128)S(1)} all-to-all(f32[32,1,128]{2,1,0:T(1,128)S(1)} %broadcast_in_dim.9), channel_id=1, replica_groups=mesh['y'=8,'c'=2,'x'=4,'z'=8] {'x','z'}, dimensions={0} | all-to-all | bytes 32768 | tf_op jit(solution)/shard_map/all_to_all | solution.py:384
  85.2 12.8 %all_to_all.26.received = f32[16,1,128]{2,1,0:T(1,128)S(1)} all-to-all(f32[16,1,128]{2,1,0:T(1,128)S(1)} %sum_spread.1), channel_id=1, replica_groups=mesh['y'=8,'c'=2,'x'=4,'z'=8] {'y','c'}, dimensions={0} | all-to-all | bytes 16384 | tf_op jit(solution)/shard_map/all_to_all | solution.py:384
  98.0 0.0 copy-done
  98.0 0.0 copy-done.1
  98.0 0.0 copy-done.2
  98.0 0.8 finish.1
  (2 shorter events, 0.0 us)
Async XLA Ops:
  7.7 23.4 %all-to-all-start = ((f32[32,16,128]{2,1,0:T(8,128)}), f32[32,16,128]{2,1,0:T(8,128)S(1)}, u32[]{:S(2)}, u32[]{:S(2)}) async-start(f32[32,16,128]{2,1,0:T(8,128)} %bitcast.1), calls=%async_computation | async-start | bytes 524288 | tf_op jit(solution)/shard_map/all_to_all | solution.py:384
  21.5 7.6 %collective-permute-start = (f32[32,256]{1,0:T(8,128)S(1)}, f32[32,256]{1,0:T(8,128)S(1)}, u32[]{:S(2)}, u32[]{:S(2)}) collective-permute-start(f32[32,256]{1,0:T(8,128)S(1)} %get-tuple-element.17.after.own_first), channel_id=1, source_target_pairs={{0,1},{1,0},{2,3},{3,2},{4,5},{5,4},{6,7},{7,6},{8,9},{9,8},{10,11... | collective-permute-start | bytes 98312 | tf_op jit(solution)/shard_map/ppermute | solution.py:413
  31.8 18.9 %all-to-all-start.1 = ((f32[16,8,128]{2,1,0:T(8,128)}), f32[16,8,128]{2,1,0:T(8,128)S(1)}, u32[]{:S(2)}, u32[]{:S(2)}) async-start(f32[16,8,128]{2,1,0:T(8,128)} %middle_send.1.after), calls=%async_computation.1 | async-start | bytes 131072 | tf_op jit(solution)/shard_map/all_to_all | solution.py:384
  51.5 46.6 %copy-start = (f32[32,512]{1,0:T(8,128)S(1)}, f32[32,512]{1,0:T(8,128)}, u32[]{:S(2)}) copy-start(f32[32,512]{1,0:T(8,128)} %direction.1) | copy-start | bytes 196612
  51.5 46.6 %copy-start.1 = (f32[32,512]{1,0:T(8,128)S(1)}, f32[32,512]{1,0:T(8,128)}, u32[]{:S(2)}) copy-start(f32[32,512]{1,0:T(8,128)} %residual.1) | copy-start | bytes 196612
  51.5 46.6 %copy-start.2 = (f32[32,512]{1,0:T(8,128)S(1)}, f32[32,512]{1,0:T(8,128)}, u32[]{:S(2)}) copy-start(f32[32,512]{1,0:T(8,128)} %solution.1) | copy-start | bytes 196612
  51.5 14.5 %all-to-all-start.2 = ((f32[32,16,128]{2,1,0:T(8,128)}), f32[32,16,128]{2,1,0:T(8,128)S(1)}, u32[]{:S(2)}, u32[]{:S(2)}) async-start(f32[32,16,128]{2,1,0:T(8,128)} %middle_return.1.after), calls=%async_computation.2 | async-start | bytes 524288 | tf_op jit(solution)/shard_map/all_to_all | solution.py:384

commit v4 on v3

--- a/solution.py
+++ b/solution.py
@@ -21,29 +21,32 @@
 highest = lax.Precision.HIGHEST
 
 
-COSINE_DEGREE = 6
-
-
-def cosine_coefficients():
+SINE_DEGREE = 4
+PEAK = math.sqrt(2.0 / RANK)
+
+
+def sine_coefficients():
     cheb = np.polynomial.chebyshev
     nodes = np.cos(np.pi * (np.arange(64) + 0.5) / 64)
-    series = cheb.chebfit(nodes, np.cos(2.0 * np.pi * np.sqrt((nodes + 1.0) / 8.0)), COSINE_DEGREE)
+    part = np.sqrt((nodes + 1.0) / 8.0)
+    series = cheb.chebfit(nodes, np.sin(np.pi * part) / part, SINE_DEGREE)
     poly = np.polynomial.Polynomial(cheb.cheb2poly(series))
     shifted = poly(np.polynomial.Polynomial([-1.0, 8.0]))
-    return [float(value) for value in shifted.coef * math.sqrt(2.0 / RANK)]
-
-
-COSINE = cosine_coefficients()
+    return [float(value) for value in shifted.coef * math.sqrt(2.0 * PEAK)]
+
+
+SINE = sine_coefficients()
 TURN = 2.0 * math.pi
 
 
 def scaled_cosine(turns):
     part = turns - jnp.round(turns)
     square = part * part
-    value = COSINE[-1] * square + COSINE[-2]
-    for coefficient in COSINE[-3::-1]:
+    value = SINE[-1] * square + SINE[-2]
+    for coefficient in SINE[-3::-1]:
         value = value * square + coefficient
-    return value
+    sine = value * part
+    return PEAK - sine * sine
 
 
 def split(value):
@@ -323,15 +326,15 @@
 
 def sum_spread_kernel(received, out):
     total = received[0]
-    for source in range(1, PTS):
+    for source in range(1, GRP):
         total = total + received[source]
-    for target in range(GRP):
+    for target in range(PTS):
         out[target] = total
 
 
 def finish_kernel(received, solution, residual, direction, solved, image, shifted, new_solution, new_residual, new_direction):
     total = received[0]
-    for source in range(1, GRP):
+    for source in range(1, PTS):
         total = total + received[source]
     row = lax.broadcasted_iota(jnp.int32, (ROWS, 128), 0)
     column = lax.broadcasted_iota(jnp.int32, (ROWS, 128), 1)
@@ -446,9 +449,9 @@
         scratch=(panel, leaf_rows, leaf_rows, pltpu.SemaphoreType.DMA((LEVELS + 2,))),
         name="image",
     )
-    gathered = exchange(jnp.broadcast_to(sums[None], (PTS, 1, 128)), ("x", "z"))
-    middle_sums = call(sum_spread_kernel, whole((GRP, 1, 128)), gathered, name="sum_spread")
-    totals = exchange(middle_sums, ("y", "c"))
+    gathered = exchange(jnp.broadcast_to(sums[None], (GRP, 1, 128)), ("y", "c"))
+    middle_sums = call(sum_spread_kernel, whole((PTS, 1, 128)), gathered, name="sum_spread")
+    totals = exchange(middle_sums, ("x", "z"))
     return call(
         finish_kernel, (rows, rows, rows), totals, solution, residual, direction, solved, image, shifted, name="finish"
     )

time: 99.4 us -> 97.5 us (0.981)
  blocking collectives: 28 us -> 26.6 us
    all_to_all x2, blocking collectives: 28 us -> 26.6 us  [exchange(): return lax.all_to_all(value, axes, 0, 0, tiled=True)]
  transfers between devices with their start and end apart: 4 -> 4, of which waited for: 4 -> 4; matrix products, arithmetic and copies ran while one was open for 0% -> 0% of each run, Pallas kernels for 16% -> 17%
where the time goes in v4:
time: 97.5 us; the launch traced here: 97 us
  starting transfers between devices  32.5 us (33%)
  Pallas kernels  29 us (30%)
  blocking collectives  26.6 us (27%)
  waiting for transfers between devices  8.2 us (8%)
    all_to_all x3, starting transfers between devices, exchange(): return lax.all_to_all(value, axes, 0, 0, tiled=True)  29.4 us
    pallas_call x9, Pallas kernels, call(): pl.pallas_call(kernel, out_shape=outs if single else tuple((pltpu.HBM(out...  29 us
    all_to_all x2, blocking collectives, exchange(): return lax.all_to_all(value, axes, 0, 0, tiled=True)  26.6 us
    all_to_all x3, waiting for transfers between devices, exchange(): return lax.all_to_all(value, axes, 0, 0, tiled=True)  7.64 us
    ppermute x1, starting transfers between devices, body(): other_first = lax.ppermute(part_first, 'z', [(n, n ^ 1) for n in range(8)])  3.14 us
  transfers between devices with their start and end apart: 4, of which 4 were waited for; matrix products, arithmetic and copies ran while one was open for 0% of the time, Pallas kernels for 17%

profile of v4, /device:TPU:1, one launch (start us, length us, event | category | flops | bytes accessed | tf_op | source)
XLA Modules:
  0.0 97.0 jit_solution(145970942598697445)
XLA Ops:
  0.6 6.7 %features.1 = (f32[9,512,256]{2,1,0:T(8,128)}, f32[32,256]{1,0:T(8,128)S(1)}, f32[512,128]{1,0:T(8,128)}) custom-call(bf16[512,768]{1,0:T(8,128)(2,1)} %emb_in.3, bf16[768,256]{1,0:T(8,128)(2,1)} %freq_in.1, f32[9,256]{1,0:T(8,128)} %phase_in.1, f32[32,512]{1,0:T(8,128)} %direction.1), custom_call_target="tpu_custom_call" | custom-call | tf_op jit(solution)/shard_map/features/pallas_call | solution.py:373
  7.3 13.7 %all-to-all-start = ((f32[32,16,128]{2,1,0:T(8,128)}), f32[32,16,128]{2,1,0:T(8,128)S(1)}, u32[]{:S(2)}, u32[]{:S(2)}) async-start(f32[32,16,128]{2,1,0:T(8,128)} %bitcast.1), calls=%async_computation | async-start | bytes 524288 | tf_op jit(solution)/shard_map/all_to_all | solution.py:387
  21.1 3.1 %collective-permute-start = (f32[32,256]{1,0:T(8,128)S(1)}, f32[32,256]{1,0:T(8,128)S(1)}, u32[]{:S(2)}, u32[]{:S(2)}) collective-permute-start(f32[32,256]{1,0:T(8,128)S(1)} %get-tuple-element.17.after.own_first), channel_id=1, source_target_pairs={{0,1},{1,0},{2,3},{3,2},{4,5},{5,4},{6,7},{7,6},{8,9},{9,8},{10,11... | collective-permute-start | bytes 98312 | tf_op jit(solution)/shard_map/ppermute | solution.py:416
  24.2 3.9 %leaf_matrix.1 = (f32[32,512]{1,0:T(8,128)S(1)}, f32[512,512]{1,0:T(8,128)S(1)}, f32[8,128]{1,0:T(8,128)S(1)}) custom-call(bf16[512,768]{1,0:T(8,128)(2,1)} %emb_in.3, f32[32,512]{1,0:T(8,128)} %direction.1, f32[32,256]{1,0:T(8,128)S(1)} %get-tuple-element.17.after.own_first), custom_call_target="tpu_custom_call" | custom-call | tf_op jit(solution)/shard_map/leaf_matrix/pallas_call | solution.py:373
  28.1 0.6 collective-permute-done.second_after.other_first
  28.6 2.1 %all-to-all-done.received = f32[32,16,128]{2,1,0:T(8,128)S(1)} async-done(((f32[32,16,128]{2,1,0:T(8,128)}), f32[32,16,128]{2,1,0:T(8,128)S(1)}, u32[]{:S(2)}, u32[]{:S(2)}) %all-to-all-start) | async-done | bytes 262176 | tf_op jit(solution)/shard_map/all_to_all | solution.py:387
  30.7 0.7 middle_send.1.after
  31.4 11.1 %all-to-all-start.1 = ((f32[16,8,128]{2,1,0:T(8,128)}), f32[16,8,128]{2,1,0:T(8,128)S(1)}, u32[]{:S(2)}, u32[]{:S(2)}) async-start(f32[16,8,128]{2,1,0:T(8,128)} %middle_send.1.after), calls=%async_computation.1 | async-start | bytes 131072 | tf_op jit(solution)/shard_map/all_to_all | solution.py:387
  42.5 4.5 %leaf_first.1 = (f32[256,256]{1,0:T(8,128)}, f32[256,256]{1,0:T(8,128)}, f32[256,256]{1,0:T(8,128)S(1)}) custom-call(f32[512,512]{1,0:T(8,128)S(1)} %get-tuple-element.20.matrix, f32[8,128]{1,0:T(8,128)S(1)} %get-tuple-element.19.first_after.largest, f32[16,8,128]{2,1,0:T(8,128)} %middle_send.1.after), custom_call_target="tpu_custom_call" | custom-call | tf_op jit(solution)/shard_map/leaf_first/pallas_call | solution.py:373
  47.0 3.3 %all-to-all-done.1.wide = f32[16,8,128]{2,1,0:T(8,128)S(1)} async-done(((f32[16,8,128]{2,1,0:T(8,128)}), f32[16,8,128]{2,1,0:T(8,128)S(1)}, u32[]{:S(2)}, u32[]{:S(2)}) %all-to-all-start.1) | async-done | bytes 65568 | tf_op jit(solution)/shard_map/all_to_all | solution.py:387
  50.3 0.8 middle_return.1.after
  51.1 0.0 copy-start
  51.1 0.0 copy-start.1
  51.1 0.0 copy-start.2
  51.1 4.5 %all-to-all-start.2 = ((f32[32,16,128]{2,1,0:T(8,128)}), f32[32,16,128]{2,1,0:T(8,128)S(1)}, u32[]{:S(2)}, u32[]{:S(2)}) async-start(f32[32,16,128]{2,1,0:T(8,128)} %middle_return.1.after), calls=%async_computation.2 | async-start | bytes 524288 | tf_op jit(solution)/shard_map/all_to_all | solution.py:387
  55.6 7.7 %leaf_second.1 = (f32[32,512]{1,0:T(8,128)S(1)}, bf16[3,512,512]{2,1,0:T(8,128)(2,1)S(1)}) custom-call(f32[256,256]{1,0:T(8,128)} %get-tuple-element.24.first_in, f32[256,256]{1,0:T(8,128)} %get-tuple-element.25.across_in, f32[256,256]{1,0:T(8,128)S(1)} %get-tuple-element.21.after.schur, f32[8,128]{1,0:T(8,128)S(1)} %get-tuple-element.19.first_after.largest, ...), custom_call_target="tpu_custom_call" | custom-call | tf_op jit(solution)/shard_map/leaf_second/pallas_call | solution.py:373
  63.2 2.3 %all-to-all-done.2 = f32[32,16,128]{2,1,0:T(8,128)S(1)} async-done(((f32[32,16,128]{2,1,0:T(8,128)}), f32[32,16,128]{2,1,0:T(8,128)S(1)}, u32[]{:S(2)}, u32[]{:S(2)}) %all-to-all-start.2) | async-done | bytes 262176 | tf_op jit(solution)/shard_map/all_to_all | solution.py:387
  65.5 4.0 %image.1 = (f32[32,512]{1,0:T(8,128)S(1)}, f32[32,512]{1,0:T(8,128)S(1)}, f32[1,128]{1,0:T(1,128)S(1)}) custom-call(f32[32,256]{1,0:T(8,128)S(1)} %get-tuple-element.17.after.own_first, f32[32,256]{1,0:T(8,128)S(1)} %collective-permute-done.second_after.other_first, f32[512,128]{1,0:T(8,128)S(1)} %bitcast.4, f32[9,512,256]{2,1,0:T(8,128)} %get-tuple-element.22.feat_in, ...), custom_call_target="tpu_custom_call" | custom-call | tf_op jit(solution)/shard_map/image/pallas_call | solution.py:373
  69.6 13.7 %all_to_all.25.received = f32[16,1,128]{2,1,0:T(1,128)S(1)} all-to-all(f32[16,1,128]{2,1,0:T(1,128)S(1)} %broadcast_in_dim.9), channel_id=1, replica_groups=mesh['y'=8,'c'=2,'x'=4,'z'=8] {'y','c'}, dimensions={0} | all-to-all | bytes 16384 | tf_op jit(solution)/shard_map/all_to_all | solution.py:387
  83.2 12.9 %all_to_all.26.received = f32[32,1,128]{2,1,0:T(1,128)S(1)} all-to-all(f32[32,1,128]{2,1,0:T(1,128)S(1)} %sum_spread.1), channel_id=1, replica_groups=mesh['y'=8,'c'=2,'x'=4,'z'=8] {'x','z'}, dimensions={0} | all-to-all | bytes 32768 | tf_op jit(solution)/shard_map/all_to_all | solution.py:387
  96.2 0.0 copy-done
  96.2 0.0 copy-done.1
  96.2 0.0 copy-done.2
  96.2 0.8 finish.1
  (2 shorter events, 0.0 us)
Async XLA Ops:
  7.3 23.4 %all-to-all-start = ((f32[32,16,128]{2,1,0:T(8,128)}), f32[32,16,128]{2,1,0:T(8,128)S(1)}, u32[]{:S(2)}, u32[]{:S(2)}) async-start(f32[32,16,128]{2,1,0:T(8,128)} %bitcast.1), calls=%async_computation | async-start | bytes 524288 | tf_op jit(solution)/shard_map/all_to_all | solution.py:387
  21.1 7.6 %collective-permute-start = (f32[32,256]{1,0:T(8,128)S(1)}, f32[32,256]{1,0:T(8,128)S(1)}, u32[]{:S(2)}, u32[]{:S(2)}) collective-permute-start(f32[32,256]{1,0:T(8,128)S(1)} %get-tuple-element.17.after.own_first), channel_id=1, source_target_pairs={{0,1},{1,0},{2,3},{3,2},{4,5},{5,4},{6,7},{7,6},{8,9},{9,8},{10,11... | collective-permute-start | bytes 98312 | tf_op jit(solution)/shard_map/ppermute | solution.py:416
  31.4 18.9 %all-to-all-start.1 = ((f32[16,8,128]{2,1,0:T(8,128)}), f32[16,8,128]{2,1,0:T(8,128)S(1)}, u32[]{:S(2)}, u32[]{:S(2)}) async-start(f32[16,8,128]{2,1,0:T(8,128)} %middle_send.1.after), calls=%async_computation.1 | async-start | bytes 131072 | tf_op jit(solution)/shard_map/all_to_all | solution.py:387
  51.1 45.1 %copy-start = (f32[32,512]{1,0:T(8,128)S(1)}, f32[32,512]{1,0:T(8,128)}, u32[]{:S(2)}) copy-start(f32[32,512]{1,0:T(8,128)} %direction.1) | copy-start | bytes 196612
  51.1 45.1 %copy-start.1 = (f32[32,512]{1,0:T(8,128)S(1)}, f32[32,512]{1,0:T(8,128)}, u32[]{:S(2)}) copy-start(f32[32,512]{1,0:T(8,128)} %residual.1) | copy-start | bytes 196612
  51.1 45.1 %copy-start.2 = (f32[32,512]{1,0:T(8,128)S(1)}, f32[32,512]{1,0:T(8,128)}, u32[]{:S(2)}) copy-start(f32[32,512]{1,0:T(8,128)} %solution.1) | copy-start | bytes 196612
  51.1 14.5 %all-to-all-start.2 = ((f32[32,16,128]{2,1,0:T(8,128)}), f32[32,16,128]{2,1,0:T(8,128)S(1)}, u32[]{:S(2)}, u32[]{:S(2)}) async-start(f32[32,16,128]{2,1,0:T(8,128)} %middle_return.1.after), calls=%async_computation.2 | async-start | bytes 524288 | tf_op jit(solution)/shard_map/all_to_all | solution.py:387

commit v5 on v4

--- a/solution.py
+++ b/solution.py
@@ -104,9 +104,11 @@
     ]
     for load in loads:
         load.start()
-    for load in loads:
+    for load in loads[:2]:
         load.wait()
     proj[...] = mm(emb[...], freq[...])
+    for load in loads[2:]:
+        load.wait()
     phase_turns = phase[...] * (1.0 / TURN)
 
     def chunk(step, carry):
@@ -197,7 +199,7 @@
         return carry
 
     lax.fori_loop(0, LEAF // CHUNK, chunk, 0)
-    near[...] = mm6(direction[...], matrix[...])
+    near[...] = six_products(planes(direction[...]), planes(matrix[...]), mm)
     sums = jnp.sum(matrix[...], axis=0, keepdims=True)
     largest = jnp.max(sums, axis=1, keepdims=True)
     largest_out[...] = jnp.broadcast_to(largest, (8, 128))

time: 97.5 us -> 97.5 us (level)
  transfers between devices with their start and end apart: 4 -> 4, of which waited for: 4 -> 4; matrix products, arithmetic and copies ran while one was open for 0% -> 0% of each run, Pallas kernels for 17% -> 16%
where the time goes in v5:
time: 97.5 us; the launch traced here: 97 us
  starting transfers between devices  32.5 us (33%)
  Pallas kernels  28.7 us (29%)
  blocking collectives  26.6 us (27%)
  waiting for transfers between devices  8.46 us (9%)
    all_to_all x3, starting transfers between devices, exchange(): return lax.all_to_all(value, axes, 0, 0, tiled=True)  29.4 us
    pallas_call x9, Pallas kernels, call(): pl.pallas_call(kernel, out_shape=outs if single else tuple((pltpu.HBM(out...  28.7 us
    all_to_all x2, blocking collectives, exchange(): return lax.all_to_all(value, axes, 0, 0, tiled=True)  26.6 us
    all_to_all x3, waiting for transfers between devices, exchange(): return lax.all_to_all(value, axes, 0, 0, tiled=True)  7.64 us
    ppermute x1, starting transfers between devices, body(): other_first = lax.ppermute(part_first, 'z', [(n, n ^ 1) for n in range(8)])  3.14 us
  transfers between devices with their start and end apart: 4, of which 4 were waited for; matrix products, arithmetic and copies ran while one was open for 0% of the time, Pallas kernels for 16%

profile of v5, /device:TPU:1, one launch (start us, length us, event | category | flops | bytes accessed | tf_op | source)
XLA Modules:
  0.0 97.0 jit_solution(11265468575081006011)
XLA Ops:
  0.6 6.7 %features.1 = (f32[9,512,256]{2,1,0:T(8,128)}, f32[32,256]{1,0:T(8,128)S(1)}, f32[512,128]{1,0:T(8,128)}) custom-call(bf16[512,768]{1,0:T(8,128)(2,1)} %emb_in.3, bf16[768,256]{1,0:T(8,128)(2,1)} %freq_in.1, f32[9,256]{1,0:T(8,128)} %phase_in.1, f32[32,512]{1,0:T(8,128)} %direction.1), custom_call_target="tpu_custom_call" | custom-call | tf_op jit(solution)/shard_map/features/pallas_call | solution.py:375
  7.3 13.7 %all-to-all-start = ((f32[32,16,128]{2,1,0:T(8,128)}), f32[32,16,128]{2,1,0:T(8,128)S(1)}, u32[]{:S(2)}, u32[]{:S(2)}) async-start(f32[32,16,128]{2,1,0:T(8,128)} %bitcast.1), calls=%async_computation | async-start | bytes 524288 | tf_op jit(solution)/shard_map/all_to_all | solution.py:389
  21.1 3.1 %collective-permute-start = (f32[32,256]{1,0:T(8,128)S(1)}, f32[32,256]{1,0:T(8,128)S(1)}, u32[]{:S(2)}, u32[]{:S(2)}) collective-permute-start(f32[32,256]{1,0:T(8,128)S(1)} %get-tuple-element.17.after.own_first), channel_id=1, source_target_pairs={{0,1},{1,0},{2,3},{3,2},{4,5},{5,4},{6,7},{7,6},{8,9},{9,8},{10,11... | collective-permute-start | bytes 98312 | tf_op jit(solution)/shard_map/ppermute | solution.py:418
  24.2 3.6 %leaf_matrix.1 = (f32[32,512]{1,0:T(8,128)S(1)}, f32[512,512]{1,0:T(8,128)S(1)}, f32[8,128]{1,0:T(8,128)S(1)}) custom-call(bf16[512,768]{1,0:T(8,128)(2,1)} %emb_in.3, f32[32,512]{1,0:T(8,128)} %direction.1, f32[32,256]{1,0:T(8,128)S(1)} %get-tuple-element.17.after.own_first), custom_call_target="tpu_custom_call" | custom-call | tf_op jit(solution)/shard_map/leaf_matrix/pallas_call | solution.py:375
  27.8 0.8 collective-permute-done.second_after.other_first
  28.6 2.1 %all-to-all-done.received = f32[32,16,128]{2,1,0:T(8,128)S(1)} async-done(((f32[32,16,128]{2,1,0:T(8,128)}), f32[32,16,128]{2,1,0:T(8,128)S(1)}, u32[]{:S(2)}, u32[]{:S(2)}) %all-to-all-start) | async-done | bytes 262176 | tf_op jit(solution)/shard_map/all_to_all | solution.py:389
  30.7 0.7 middle_send.1.after
  31.4 11.1 %all-to-all-start.1 = ((f32[16,8,128]{2,1,0:T(8,128)}), f32[16,8,128]{2,1,0:T(8,128)S(1)}, u32[]{:S(2)}, u32[]{:S(2)}) async-start(f32[16,8,128]{2,1,0:T(8,128)} %middle_send.1.after), calls=%async_computation.1 | async-start | bytes 131072 | tf_op jit(solution)/shard_map/all_to_all | solution.py:389
  42.5 4.5 %leaf_first.1 = (f32[256,256]{1,0:T(8,128)}, f32[256,256]{1,0:T(8,128)}, f32[256,256]{1,0:T(8,128)S(1)}) custom-call(f32[512,512]{1,0:T(8,128)S(1)} %get-tuple-element.20.matrix, f32[8,128]{1,0:T(8,128)S(1)} %get-tuple-element.19.first_after.largest, f32[16,8,128]{2,1,0:T(8,128)} %middle_send.1.after), custom_call_target="tpu_custom_call" | custom-call | tf_op jit(solution)/shard_map/leaf_first/pallas_call | solution.py:375
  47.0 3.3 %all-to-all-done.1.wide = f32[16,8,128]{2,1,0:T(8,128)S(1)} async-done(((f32[16,8,128]{2,1,0:T(8,128)}), f32[16,8,128]{2,1,0:T(8,128)S(1)}, u32[]{:S(2)}, u32[]{:S(2)}) %all-to-all-start.1) | async-done | bytes 65568 | tf_op jit(solution)/shard_map/all_to_all | solution.py:389
  50.3 0.8 middle_return.1.after
  51.1 0.0 copy-start
  51.1 0.0 copy-start.1
  51.1 0.0 copy-start.2
  51.1 4.5 %all-to-all-start.2 = ((f32[32,16,128]{2,1,0:T(8,128)}), f32[32,16,128]{2,1,0:T(8,128)S(1)}, u32[]{:S(2)}, u32[]{:S(2)}) async-start(f32[32,16,128]{2,1,0:T(8,128)} %middle_return.1.after), calls=%async_computation.2 | async-start | bytes 524288 | tf_op jit(solution)/shard_map/all_to_all | solution.py:389
  55.6 7.7 %leaf_second.1 = (f32[32,512]{1,0:T(8,128)S(1)}, bf16[3,512,512]{2,1,0:T(8,128)(2,1)S(1)}) custom-call(f32[256,256]{1,0:T(8,128)} %get-tuple-element.24.first_in, f32[256,256]{1,0:T(8,128)} %get-tuple-element.25.across_in, f32[256,256]{1,0:T(8,128)S(1)} %get-tuple-element.21.after.schur, f32[8,128]{1,0:T(8,128)S(1)} %get-tuple-element.19.first_after.largest, ...), custom_call_target="tpu_custom_call" | custom-call | tf_op jit(solution)/shard_map/leaf_second/pallas_call | solution.py:375
  63.2 2.3 %all-to-all-done.2 = f32[32,16,128]{2,1,0:T(8,128)S(1)} async-done(((f32[32,16,128]{2,1,0:T(8,128)}), f32[32,16,128]{2,1,0:T(8,128)S(1)}, u32[]{:S(2)}, u32[]{:S(2)}) %all-to-all-start.2) | async-done | bytes 262176 | tf_op jit(solution)/shard_map/all_to_all | solution.py:389
  65.5 4.0 %image.1 = (f32[32,512]{1,0:T(8,128)S(1)}, f32[32,512]{1,0:T(8,128)S(1)}, f32[1,128]{1,0:T(1,128)S(1)}) custom-call(f32[32,256]{1,0:T(8,128)S(1)} %get-tuple-element.17.after.own_first, f32[32,256]{1,0:T(8,128)S(1)} %collective-permute-done.second_after.other_first, f32[512,128]{1,0:T(8,128)S(1)} %bitcast.4, f32[9,512,256]{2,1,0:T(8,128)} %get-tuple-element.22.feat_in, ...), custom_call_target="tpu_custom_call" | custom-call | tf_op jit(solution)/shard_map/image/pallas_call | solution.py:375
  69.6 13.7 %all_to_all.25.received = f32[16,1,128]{2,1,0:T(1,128)S(1)} all-to-all(f32[16,1,128]{2,1,0:T(1,128)S(1)} %broadcast_in_dim.9), channel_id=1, replica_groups=mesh['y'=8,'c'=2,'x'=4,'z'=8] {'y','c'}, dimensions={0} | all-to-all | bytes 16384 | tf_op jit(solution)/shard_map/all_to_all | solution.py:389
  83.2 12.9 %all_to_all.26.received = f32[32,1,128]{2,1,0:T(1,128)S(1)} all-to-all(f32[32,1,128]{2,1,0:T(1,128)S(1)} %sum_spread.1), channel_id=1, replica_groups=mesh['y'=8,'c'=2,'x'=4,'z'=8] {'x','z'}, dimensions={0} | all-to-all | bytes 32768 | tf_op jit(solution)/shard_map/all_to_all | solution.py:389
  96.2 0.0 copy-done
  96.2 0.0 copy-done.1
  96.2 0.0 copy-done.2
  96.2 0.8 finish.1
  (2 shorter events, 0.0 us)
Async XLA Ops:
  7.3 23.4 %all-to-all-start = ((f32[32,16,128]{2,1,0:T(8,128)}), f32[32,16,128]{2,1,0:T(8,128)S(1)}, u32[]{:S(2)}, u32[]{:S(2)}) async-start(f32[32,16,128]{2,1,0:T(8,128)} %bitcast.1), calls=%async_computation | async-start | bytes 524288 | tf_op jit(solution)/shard_map/all_to_all | solution.py:389
  21.1 7.6 %collective-permute-start = (f32[32,256]{1,0:T(8,128)S(1)}, f32[32,256]{1,0:T(8,128)S(1)}, u32[]{:S(2)}, u32[]{:S(2)}) collective-permute-start(f32[32,256]{1,0:T(8,128)S(1)} %get-tuple-element.17.after.own_first), channel_id=1, source_target_pairs={{0,1},{1,0},{2,3},{3,2},{4,5},{5,4},{6,7},{7,6},{8,9},{9,8},{10,11... | collective-permute-start | bytes 98312 | tf_op jit(solution)/shard_map/ppermute | solution.py:418
  31.4 18.9 %all-to-all-start.1 = ((f32[16,8,128]{2,1,0:T(8,128)}), f32[16,8,128]{2,1,0:T(8,128)S(1)}, u32[]{:S(2)}, u32[]{:S(2)}) async-start(f32[16,8,128]{2,1,0:T(8,128)} %middle_send.1.after), calls=%async_computation.1 | async-start | bytes 131072 | tf_op jit(solution)/shard_map/all_to_all | solution.py:389
  51.1 45.1 %copy-start = (f32[32,512]{1,0:T(8,128)S(1)}, f32[32,512]{1,0:T(8,128)}, u32[]{:S(2)}) copy-start(f32[32,512]{1,0:T(8,128)} %direction.1) | copy-start | bytes 196612
  51.1 45.1 %copy-start.1 = (f32[32,512]{1,0:T(8,128)S(1)}, f32[32,512]{1,0:T(8,128)}, u32[]{:S(2)}) copy-start(f32[32,512]{1,0:T(8,128)} %residual.1) | copy-start | bytes 196612
  51.1 45.1 %copy-start.2 = (f32[32,512]{1,0:T(8,128)S(1)}, f32[32,512]{1,0:T(8,128)}, u32[]{:S(2)}) copy-start(f32[32,512]{1,0:T(8,128)} %solution.1) | copy-start | bytes 196612
  51.1 14.5 %all-to-all-start.2 = ((f32[32,16,128]{2,1,0:T(8,128)}), f32[32,16,128]{2,1,0:T(8,128)S(1)}, u32[]{:S(2)}, u32[]{:S(2)}) async-start(f32[32,16,128]{2,1,0:T(8,128)} %middle_return.1.after), calls=%async_computation.2 | async-start | bytes 524288 | tf_op jit(solution)/shard_map/all_to_all | solution.py:389
